TPU v7x, 128 devices: a whole 4x4x4 slice. The times are simulated.
128 devices in a mesh: chan: 8 (over y_hi, z), tm: 16 (over x, y_lo, core).
Axes of the slice: x: 4, y: 4 (y_hi: 2, y_lo: 2; y = y_hi * 2 + y_lo), z: 4, core: 2. Of those that a mesh axis runs over, the one named last changes fastest.
Arguments:
- raw_strain: float32 [512, 16384], P('chan', 'tm'), may hold values from -6 to 6
- whitening: float32 [1024], replicated, may hold values from -0.1875 to 0.1875
- block_mask: int32 [8, 8], replicated, may hold values from 0 to 1, as said below
- old_stack: float32 [32, 512, 512], P('tm', 'chan'), may hold values from -6 to 6
Outputs:
- new_stack: float32 [32, 512, 512], P('tm', 'chan')
Inputs may be any that keep to these rules, and one draw needn't show every extreme that they name: block_mask[a, b] is 1 exactly where (b - a) mod 8 is below a reach of row a, each reach at least 1, and 0 elsewhere.
All inputs are finite; a program needn't handle non-finite values.
Results may differ from a plain program's by a relative error of at most 0.0018.
Values may be sent and summed in bfloat16 or wider, within the bound.
No kernel may reach another device: no remote copies, remote signals or barrier semaphores. Data moves between devices by JAX's collectives and lax.ppermute only.
A program may use at most 64 MiB of HBM per device.

v0:
```python
import functools

import jax
import jax.numpy as jnp
from jax import lax
from jax.experimental import pallas as pl
from jax.experimental.pallas import tpu as pltpu
from jax.sharding import Mesh, PartitionSpec as P


CHAN = ("yh", "z")
TIME = ("x", "yl", "c")
OWNERS = ("yh", "x", "yl")
VMEM = pl.BlockSpec(memory_space=pltpu.VMEM)
SMEM = pl.BlockSpec(memory_space=pltpu.SMEM)
NT = (((1,), (1,)), ((), ()))
TILE = 256
PAD = 128
MIB = 1 << 20


def call(kernel, out_shape, operands, mib, flops, specs=None):
    return pl.pallas_call(
        kernel,
        out_shape=out_shape,
        in_specs=specs or [VMEM] * len(operands),
        out_specs=jax.tree.map(lambda _: VMEM, out_shape),
        compiler_params=pltpu.CompilerParams(vmem_limit_bytes=mib * MIB),
        cost_estimate=pl.CostEstimate(flops=flops, bytes_accessed=MIB, transcendentals=0),
    )(*operands)


def split(value):
    high = value.astype(jnp.bfloat16)
    return high, (value - high.astype(jnp.float32)).astype(jnp.bfloat16)


def prepare_kernel(taps_ref, own_ref, high_ref, low_ref, own_high_ref, own_low_ref):
    own_high_ref[...], own_low_ref[...] = split(own_ref[...])
    rows, width = high_ref.shape
    taps = taps_ref[...]
    row = jnp.concatenate([taps, jnp.zeros((1, width - taps.shape[1]), jnp.float32)], axis=1)
    matrix = pltpu.roll(jnp.broadcast_to(row, (rows, width)), 0, 1, stride=1, stride_axis=0)
    high_ref[...], low_ref[...] = split(matrix)


def prepare(whitening, own):
    matrix = jax.ShapeDtypeStruct((TILE, whitening.shape[0] + TILE), jnp.bfloat16)
    part = jax.ShapeDtypeStruct(own.shape, jnp.bfloat16)
    shapes = (matrix, matrix, part, part)
    return call(prepare_kernel, shapes, (whitening[None, :], own), 8, 10**9)


def filter_kernel(
    half_taps, place_ref, beside_ref, across_ref, mat_high_ref, mat_low_ref, own_high_ref, own_low_ref, mine_ref, own_ref
):
    channels, seg_len = own_ref.shape
    width = mat_high_ref.shape[1]
    blocks = seg_len // TILE + 1
    lower = place_ref[0] == 0
    reach = half_taps + PAD
    across = across_ref[...]
    low = split(jnp.where(lower, across, beside_ref[:, seg_len - reach :]))
    high = split(jnp.where(lower, beside_ref[:, :half_taps], across[:, :half_taps]))

    def stacked(before, own, after):
        zeros = jnp.zeros((channels, TILE - PAD), jnp.bfloat16)
        padded = jnp.concatenate([zeros, before, own, after], axis=1)
        return jnp.concatenate(
            [padded[:, b * TILE : b * TILE + width] for b in range(blocks)], axis=0
        )

    x_high = stacked(low[0], own_high_ref[...], high[0])
    x_low = stacked(low[1], own_low_ref[...], high[1])
    dot = functools.partial(lax.dot_general, dimension_numbers=NT, preferred_element_type=jnp.float32)
    total = dot(x_low, mat_high_ref[...]) + dot(x_high, mat_low_ref[...])
    total = total + dot(x_high, mat_high_ref[...])
    before = total[:channels, TILE - PAD :]
    before = jnp.where(place_ref[1] == 0, jnp.zeros_like(before), before)
    mine_ref[:, :PAD] = before.astype(jnp.bfloat16)
    for b in range(1, blocks):
        piece = total[b * channels : (b + 1) * channels].astype(jnp.bfloat16)
        mine_ref[:, PAD + (b - 1) * TILE : PAD + b * TILE] = piece
        own_ref[:, (b - 1) * TILE : b * TILE] = piece


def filter_segment(place, beside, across, prepared, half_taps):
    channels, seg_len = beside.shape
    return call(
        functools.partial(filter_kernel, half_taps),
        (
            jax.ShapeDtypeStruct((channels, PAD + seg_len), jnp.bfloat16),
            jax.ShapeDtypeStruct((channels, seg_len), jnp.bfloat16),
        ),
        (place, beside, across, *prepared),
        12,
        10**9,
        [SMEM] + [VMEM] * 6,
    )


def rows_kernel(lag_count, place_ref, mine_ref, theirs_ref, rows_ref):
    channels = mine_ref.shape[0]
    core = place_ref[0]
    mine, theirs = mine_ref[...], theirs_ref[...]
    first = jnp.where(core == 0, mine, theirs)
    second = jnp.where(core == 0, theirs, mine)
    both = jnp.concatenate([first, second[:, PAD:]], axis=1)
    both = jnp.where(core == 0, both, pltpu.roll(both, 2, 1))
    for index in range(lag_count):
        lag = 4 * (index // 2) + index % 2
        moved = both if lag == 0 else pltpu.roll(both, lag, 1)
        rows_ref[index * channels : (index + 1) * channels, :] = moved[:, PAD:]


def lagged_rows(place, mine, theirs, lag_count):
    channels, width = mine.shape
    return call(
        functools.partial(rows_kernel, lag_count),
        jax.ShapeDtypeStruct((lag_count * channels, 2 * (width - PAD)), jnp.bfloat16),
        (place, mine, theirs),
        8,
        2 * 10**9,
        [SMEM, VMEM, VMEM],
    )


def correlate_kernel(place_ref, *refs):
    *piece_refs, mine_ref, other_ref, out_ref, cols_ref = refs
    core, yh = place_ref[0], place_ref[2]
    half = len(piece_refs) // 2
    channels, seg_len = piece_refs[0].shape
    side = pl.program_id(0)

    @pl.when(side == 0)
    def _():
        for index in range(half):
            at = pl.ds(pl.multiple_of(place_ref[3 + index] * channels, channels), channels)
            for k in range(2):
                begin = pl.multiple_of((core if k == 0 else 1 - core) * seg_len, seg_len)
                cols_ref[at, pl.ds(begin, seg_len)] = piece_refs[2 * index + k][...]

    def fill(rows_ref):
        out_ref[0] = lax.dot_general(
            rows_ref[...], cols_ref[...], NT, preferred_element_type=jnp.float32
        ).astype(jnp.bfloat16)

    pl.when(side == yh)(lambda: fill(mine_ref))
    pl.when(side != yh)(lambda: fill(other_ref))


def correlate(place, pieces, mine_rows, other_rows):
    channels, seg_len = pieces[0].shape
    width = channels * (len(pieces) // 2)
    rows = mine_rows.shape[0]
    return pl.pallas_call(
        correlate_kernel,
        grid=(2,),
        out_shape=jax.ShapeDtypeStruct((2, rows, width), jnp.bfloat16),
        in_specs=[SMEM] + [VMEM] * (len(pieces) + 2),
        out_specs=pl.BlockSpec((1, rows, width), lambda side: (side, 0, 0)),
        scratch_shapes=[pltpu.VMEM((width, 2 * seg_len), jnp.bfloat16)],
        compiler_params=pltpu.CompilerParams(vmem_limit_bytes=20 * MIB),
        cost_estimate=pl.CostEstimate(flops=4 * 10**9, bytes_accessed=MIB, transcendentals=0),
        name="correlate",
    )(place, *pieces, mine_rows, other_rows)


def stack_kernel(parts_ref, weights_ref, old_ref, out_ref):
    width = parts_ref.shape[-1]
    count = parts_ref.shape[1]
    for side in range(2):
        at = slice(side * width, (side + 1) * width)
        total = parts_ref[side, 0].astype(jnp.float32)
        for k in range(1, count):
            total = total + parts_ref[side, k].astype(jnp.float32)
        out_ref[:, at] = old_ref[:, at] + total * weights_ref[:, at]


def stack(parts, weights, old_stack):
    lags, channels, width = old_stack.shape
    parts = parts.reshape(2, -1, lags * channels, parts.shape[-1])
    shape = jax.ShapeDtypeStruct((lags * channels, width), jnp.float32)
    old = old_stack.reshape(lags * channels, width)
    return call(stack_kernel, shape, (parts, weights, old), 8, 10**8).reshape(old_stack.shape)


def turned(value, axis, distance):
    size = lax.axis_size(axis)
    return lax.ppermute(value, axis, [(i, (i + distance) % size) for i in range(size)])


def shards(raw_strain, whitening, block_mask, old_stack):
    channels, seg_len = raw_strain.shape
    half_taps = whitening.shape[0] // 2
    segments = lax.axis_size(TIME)
    lags = old_stack.shape[0]
    core, z, yh, zs = lax.axis_index("c"), lax.axis_index("z"), lax.axis_index("yh"), lax.axis_size("z")
    distances = (0, 2, 1, 3)
    place = [core, lax.axis_index(TIME), yh] + [(z - d) % zs for d in distances]
    place = jnp.stack(place).astype(jnp.int32)
    reach = half_taps + PAD
    edge = jnp.where(core == 0, raw_strain[:, :reach], raw_strain[:, seg_len - reach :])
    pairs = [(i, i + 1) for i in range(1, segments - 1, 2)]
    across = lax.ppermute(edge, TIME, pairs + [(b, a) for a, b in pairs])
    beside = turned(raw_strain, "c", 1)
    prepared = prepare(whitening, raw_strain)
    mine, own = filter_segment(place, beside, across, prepared, half_taps)
    other = turned(mine, "yh", 1)
    pieces = []
    for d in distances:
        piece = turned(own, "z", d) if d else own
        pieces += [piece, turned(piece, "c", 1)]
    lag_count = lags * segments // 2
    mine_swapped = turned(mine, "c", 1)
    other_swapped = turned(other, "c", 1)
    mine_rows = lagged_rows(place, mine, mine_swapped, lag_count)
    other_rows = lagged_rows(place, other, other_swapped, lag_count)
    partial = correlate(place, pieces, mine_rows, other_rows)
    partial = partial.reshape(segments, lags, channels, -1)
    received = lax.all_to_all(partial, OWNERS, 0, 0)
    scaling = float(seg_len * segments) ** (-0.5)
    weights = jnp.repeat(block_mask[yh * zs + z].astype(jnp.float32) * scaling, channels)[None, :]
    return stack(received, weights, old_stack)


def solution(mesh):
    fine = Mesh(mesh.devices.reshape(2, 4, 4, 2, 2), CHAN + TIME)
    in_specs = (P(CHAN, TIME), P(), P(), P(TIME, CHAN, None))
    out_specs = P(TIME, CHAN, None)
    return jax.shard_map(shards, mesh=fine, in_specs=in_specs, out_specs=out_specs, check_vma=False)
```

profile of v0, /device:TPU:0, one launch (start us, length us, event | category | flops | bytes accessed | tf_op | source)
XLA Modules:
  0.0 59.1 jit_solution(13345418660453443415)
XLA Ops:
  0.0 1.0 %slice_select_fusion = f32[64,640]{1,0:T(8,128)S(1)} fusion(f32[64,1024]{1,0:T(8,128)} %own_ref.1, pred[]{:T(512)S(6)} %eq.8), kind=kLoop, calls=%fused_computation | loop fusion | flops 40960 | bytes 491521 | tf_op jit(solution)/shard_map/jit(_where)/select_n | solution.py:203
  1.0 0.7 %collective-permute-start.1 = (f32[64,640]{1,0:T(8,128)S(1)}, f32[64,640]{1,0:T(8,128)S(1)}, u32[]{:S(2)}, u32[]{:S(2)}) collective-permute-start(f32[64,640]{1,0:T(8,128)S(1)} %slice_select_fusion), channel_id=1, source_target_pairs={{1,2},{3,4},{5,6},{7,8},{9,10},{11,12},{13,14},{2,1},{4,3},{6,5},{... | collective-permute-start | bytes 491528 | tf_op jit(solution)/shard_map/ppermute | solution.py:205
  1.8 0.1 stack.31.place_ref
  1.9 0.9 %copy-done = f32[64,1024]{1,0:T(8,128)S(1)} copy-done((f32[64,1024]{1,0:T(8,128)S(1)}, f32[64,1024]{1,0:T(8,128)}, u32[]{:S(2)}) %copy-start) | copy-done | bytes 262168
  2.8 0.7 %copy-done.2 = f32[1024]{0:T(1024)S(1)} copy-done((f32[1024]{0:T(1024)S(1)}, f32[1024]{0:T(1024)}, u32[]{:S(2)}) %copy-start.2) | copy-done | bytes 4120
  3.5 0.3 shard_map.46
  3.8 1.4 %shard_map.47 = (bf16[64,1152]{1,0:T(8,128)(2,1)S(1)}, bf16[64,1024]{1,0:T(8,128)(2,1)S(1)}) custom-call(s32[7]{0:T(128)S(1)} %stack.31.place_ref, f32[64,1024]{1,0:T(8,128)S(1)} %collective-permute-done.beside_ref, f32[64,640]{1,0:T(8,128)S(1)} %collective-permute-done.1.across_ref, bf16[256,1280]{1,0:T(8,128)(2,1)S(1)} %get-tuple-element.11.mat_high_ref, ...), custom_call_target="tpu_custom_call" | custom-call | flops 1000000000 | bytes 1048576 | tf_op jit(solution)/shard_map/pallas_call | solution.py:23
  5.2 3.4 %collective-permute-start.10 = (bf16[64,1152]{1,0:T(8,128)(2,1)S(1)}, bf16[64,1152]{1,0:T(8,128)(2,1)S(1)}, u32[]{:S(2)}, u32[]{:S(2)}) collective-permute-start(bf16[64,1152]{1,0:T(8,128)(2,1)S(1)} %get-tuple-element.16.mine_ref), channel_id=1, source_target_pairs={{0,64},{64,0},{1,65},{65,1},{2,66},{66,2},{3,67},{67,3},{4,68},{68... | collective-permute-start | bytes 442376 | tf_op jit(solution)/shard_map/ppermute | solution.py:190
  8.6 4.1 %collective-permute-start.9 = (bf16[64,1152]{1,0:T(8,128)(2,1)S(1)}, bf16[64,1152]{1,0:T(8,128)(2,1)S(1)}, u32[]{:S(2)}, u32[]{:S(2)}) collective-permute-start(bf16[64,1152]{1,0:T(8,128)(2,1)S(1)} %get-tuple-element.16.mine_ref), channel_id=1, source_target_pairs={{0,1},{1,0},{2,3},{3,2},{4,5},{5,4},{6,7},{7,6},{8,9},{9,8},{10,11... | collective-permute-start | bytes 442376 | tf_op jit(solution)/shard_map/ppermute | solution.py:190
  12.7 3.9 %collective-permute-start.3 = (bf16[64,1024]{1,0:T(8,128)(2,1)S(1)}, bf16[64,1024]{1,0:T(8,128)(2,1)S(1)}, u32[]{:S(2)}, u32[]{:S(2)}) collective-permute-start(bf16[64,1024]{1,0:T(8,128)(2,1)S(1)} %get-tuple-element.15.refs_0_), channel_id=1, source_target_pairs={{0,32},{16,48},{32,0},{48,16},{1,33},{17,49},{33,1},{49,17},{2,34}... | collective-permute-start | bytes 393224 | tf_op jit(solution)/shard_map/ppermute | solution.py:190
  16.5 1.0 %collective-permute-start.5 = (bf16[64,1024]{1,0:T(8,128)(2,1)S(1)}, bf16[64,1024]{1,0:T(8,128)(2,1)S(1)}, u32[]{:S(2)}, u32[]{:S(2)}) collective-permute-start(bf16[64,1024]{1,0:T(8,128)(2,1)S(1)} %get-tuple-element.15.refs_0_), channel_id=1, source_target_pairs={{0,16},{16,32},{32,48},{48,0},{1,17},{17,33},{33,49},{49,1},{2,18}... | collective-permute-start | bytes 393224 | tf_op jit(solution)/shard_map/ppermute | solution.py:190
  17.6 2.2 %collective-permute-start.7 = (bf16[64,1024]{1,0:T(8,128)(2,1)S(1)}, bf16[64,1024]{1,0:T(8,128)(2,1)S(1)}, u32[]{:S(2)}, u32[]{:S(2)}) collective-permute-start(bf16[64,1024]{1,0:T(8,128)(2,1)S(1)} %get-tuple-element.15.refs_0_), channel_id=1, source_target_pairs={{0,48},{16,0},{32,16},{48,32},{1,49},{17,1},{33,17},{49,33},{2,50}... | collective-permute-start | bytes 393224 | tf_op jit(solution)/shard_map/ppermute | solution.py:190
  19.8 1.1 %collective-permute-done.3.refs_2_ = bf16[64,1024]{1,0:T(8,128)(2,1)S(1)} collective-permute-done((bf16[64,1024]{1,0:T(8,128)(2,1)S(1)}, bf16[64,1024]{1,0:T(8,128)(2,1)S(1)}, u32[]{:S(2)}, u32[]{:S(2)}) %collective-permute-start.3) | collective-permute-done | bytes 131104 | tf_op jit(solution)/shard_map/ppermute | solution.py:190
  20.9 2.4 %collective-permute-done.5.refs_4_ = bf16[64,1024]{1,0:T(8,128)(2,1)S(1)} collective-permute-done((bf16[64,1024]{1,0:T(8,128)(2,1)S(1)}, bf16[64,1024]{1,0:T(8,128)(2,1)S(1)}, u32[]{:S(2)}, u32[]{:S(2)}) %collective-permute-start.5) | collective-permute-done | bytes 131104 | tf_op jit(solution)/shard_map/ppermute | solution.py:190
  23.3 0.5 collective-permute-done.7.refs_6_
  23.8 0.5 collective-permute-start.8
  24.3 0.1 collective-permute-start.11
  24.3 1.8 %shard_map.48.refs_8_ = bf16[1024,2048]{1,0:T(8,128)(2,1)S(1)} custom-call(s32[7]{0:T(128)S(1)} %stack.31.place_ref, bf16[64,1152]{1,0:T(8,128)(2,1)S(1)} %get-tuple-element.16.mine_ref, bf16[64,1152]{1,0:T(8,128)(2,1)S(1)} %collective-permute-done.9.theirs_ref), custom_call_target="tpu_custom_call" | custom-call | flops 2000000000 | bytes 1048576 | tf_op jit(solution)/shard_map/pallas_call | solution.py:23
  26.2 1.8 %shard_map.49.refs_9_ = bf16[1024,2048]{1,0:T(8,128)(2,1)S(1)} custom-call(s32[7]{0:T(128)S(1)} %stack.31.place_ref, bf16[64,1152]{1,0:T(8,128)(2,1)S(1)} %collective-permute-done.10.mine_ref, bf16[64,1152]{1,0:T(8,128)(2,1)S(1)} %collective-permute-done.11.theirs_ref), custom_call_target="tpu_custom_call" | custom-call | flops 2000000000 | bytes 1048576 | tf_op jit(solution)/shard_map/pallas_call | solution.py:23
  28.1 4.1 %correlate.1 = bf16[2,1024,256]{2,1,0:T(8,128)(2,1)} custom-call(s32[7]{0:T(128)S(1)} %stack.31.place_ref, bf16[64,1024]{1,0:T(8,128)(2,1)S(1)} %get-tuple-element.15.refs_0_, bf16[64,1024]{1,0:T(8,128)(2,1)S(1)} %collective-permute-done.2.refs_1_, bf16[64,1024]{1,0:T(8,128)(2,1)S(1)} %collective-permute-done.3.refs_2_, ...), custom_call_target="tpu_custom_call" | custom-call | flops 4000000000 | bytes 1048576 | tf_op jit(solution)/shard_map/correlate/pallas_call | solution.py:156
  32.2 7.1 %all-to-all-start = ((bf16[16,2,64,256]{3,2,1,0:T(8,128)(2,1)}), bf16[16,2,64,256]{3,2,1,0:T(8,128)(2,1)S(1)}, u32[]{:S(2)}, u32[]{:S(2)}) async-start(bf16[16,2,64,256]{3,2,1,0:T(8,128)(2,1)} %bitcast.8), calls=%async_computation | async-start | bytes 2097152 | tf_op jit(solution)/shard_map/all_to_all | solution.py:221
  39.3 0.7 %multiply_bitcast_fusion = f32[8]{0:T(128)S(1)} fusion(s32[8,8]{1,0:T(8,128)} %param.6, s32[]{:T(128)S(6)} %select_n.36), kind=kLoop, calls=%fused_computation.1 | loop fusion | flops 16 | bytes 68 | tf_op jit(solution)/shard_map/mul | solution.py:223
  40.2 18.1 %all-to-all-done = bf16[16,2,64,256]{3,2,1,0:T(8,128)(2,1)S(1)} async-done(((bf16[16,2,64,256]{3,2,1,0:T(8,128)(2,1)}), bf16[16,2,64,256]{3,2,1,0:T(8,128)(2,1)S(1)}, u32[]{:S(2)}, u32[]{:S(2)}) %all-to-all-start) | async-done | bytes 1048608 | tf_op jit(solution)/shard_map/all_to_all | solution.py:221
  58.2 0.9 %shard_map.50 = f32[128,512]{1,0:T(8,128)} custom-call(bf16[2,8,128,256]{3,2,1,0:T(8,128)(2,1)S(1)} %bitcast.14, f32[1,512]{1,0:T(1,128)S(1)} %broadcast_in_dim_reshape.3.weights_ref, f32[128,512]{1,0:T(8,128)S(1)} %bitcast.15), custom_call_target="tpu_custom_call" | custom-call | flops 100000000 | bytes 1048576 | tf_op jit(solution)/shard_map/pallas_call | solution.py:23
  (19 shorter events, 0.2 us)
Async XLA Ops:
  0.0 3.8 %collective-permute-start = (f32[64,1024]{1,0:T(8,128)}, f32[64,1024]{1,0:T(8,128)S(1)}, u32[]{:S(2)}, u32[]{:S(2)}) collective-permute-start(f32[64,1024]{1,0:T(8,128)} %own_ref.1), channel_id=1, source_target_pairs={{0,1},{1,0},{2,3},{3,2},{4,5},{5,4},{6,7},{7,6},{8,9},{9,8},{10,11... | collective-permute-start | bytes 786440 | tf_op jit(solution)/shard_map/ppermute | solution.py:190
  1.0 2.8 %collective-permute-start.1 = (f32[64,640]{1,0:T(8,128)S(1)}, f32[64,640]{1,0:T(8,128)S(1)}, u32[]{:S(2)}, u32[]{:S(2)}) collective-permute-start(f32[64,640]{1,0:T(8,128)S(1)} %slice_select_fusion), channel_id=1, source_target_pairs={{1,2},{3,4},{5,6},{7,8},{9,10},{11,12},{13,14},{2,1},{4,3},{6,5},{... | collective-permute-start | bytes 491528 | tf_op jit(solution)/shard_map/ppermute | solution.py:205
  1.9 1.0 %copy-start = (f32[64,1024]{1,0:T(8,128)S(1)}, f32[64,1024]{1,0:T(8,128)}, u32[]{:S(2)}) copy-start(f32[64,1024]{1,0:T(8,128)} %own_ref.1) | copy-start | bytes 786436
  2.8 0.7 %copy-start.2 = (f32[1024]{0:T(1024)S(1)}, f32[1024]{0:T(1024)}, u32[]{:S(2)}) copy-start(f32[1024]{0:T(1024)} %param.5) | copy-start | bytes 12292
  5.2 18.6 %collective-permute-start.10 = (bf16[64,1152]{1,0:T(8,128)(2,1)S(1)}, bf16[64,1152]{1,0:T(8,128)(2,1)S(1)}, u32[]{:S(2)}, u32[]{:S(2)}) collective-permute-start(bf16[64,1152]{1,0:T(8,128)(2,1)S(1)} %get-tuple-element.16.mine_ref), channel_id=1, source_target_pairs={{0,64},{64,0},{1,65},{65,1},{2,66},{66,2},{3,67},{67,3},{4,68},{68... | collective-permute-start | bytes 442376 | tf_op jit(solution)/shard_map/ppermute | solution.py:190
  8.6 15.7 %collective-permute-start.9 = (bf16[64,1152]{1,0:T(8,128)(2,1)S(1)}, bf16[64,1152]{1,0:T(8,128)(2,1)S(1)}, u32[]{:S(2)}, u32[]{:S(2)}) collective-permute-start(bf16[64,1152]{1,0:T(8,128)(2,1)S(1)} %get-tuple-element.16.mine_ref), channel_id=1, source_target_pairs={{0,1},{1,0},{2,3},{3,2},{4,5},{5,4},{6,7},{7,6},{8,9},{9,8},{10,11... | collective-permute-start | bytes 442376 | tf_op jit(solution)/shard_map/ppermute | solution.py:190
  12.7 8.2 %collective-permute-start.3 = (bf16[64,1024]{1,0:T(8,128)(2,1)S(1)}, bf16[64,1024]{1,0:T(8,128)(2,1)S(1)}, u32[]{:S(2)}, u32[]{:S(2)}) collective-permute-start(bf16[64,1024]{1,0:T(8,128)(2,1)S(1)} %get-tuple-element.15.refs_0_), channel_id=1, source_target_pairs={{0,32},{16,48},{32,0},{48,16},{1,33},{17,49},{33,1},{49,17},{2,34}... | collective-permute-start | bytes 393224 | tf_op jit(solution)/shard_map/ppermute | solution.py:190
  16.5 6.7 %collective-permute-start.5 = (bf16[64,1024]{1,0:T(8,128)(2,1)S(1)}, bf16[64,1024]{1,0:T(8,128)(2,1)S(1)}, u32[]{:S(2)}, u32[]{:S(2)}) collective-permute-start(bf16[64,1024]{1,0:T(8,128)(2,1)S(1)} %get-tuple-element.15.refs_0_), channel_id=1, source_target_pairs={{0,16},{16,32},{32,48},{48,0},{1,17},{17,33},{33,49},{49,1},{2,18}... | collective-permute-start | bytes 393224 | tf_op jit(solution)/shard_map/ppermute | solution.py:190
  17.6 6.2 %collective-permute-start.7 = (bf16[64,1024]{1,0:T(8,128)(2,1)S(1)}, bf16[64,1024]{1,0:T(8,128)(2,1)S(1)}, u32[]{:S(2)}, u32[]{:S(2)}) collective-permute-start(bf16[64,1024]{1,0:T(8,128)(2,1)S(1)} %get-tuple-element.15.refs_0_), channel_id=1, source_target_pairs={{0,48},{16,0},{32,16},{48,32},{1,49},{17,1},{33,17},{49,33},{2,50}... | collective-permute-start | bytes 393224 | tf_op jit(solution)/shard_map/ppermute | solution.py:190
  20.9 7.2 %collective-permute-start.2 = (bf16[64,1024]{1,0:T(8,128)(2,1)S(1)}, bf16[64,1024]{1,0:T(8,128)(2,1)S(1)}, u32[]{:S(2)}, u32[]{:S(2)}) collective-permute-start(bf16[64,1024]{1,0:T(8,128)(2,1)S(1)} %get-tuple-element.15.refs_0_), channel_id=1, source_target_pairs={{0,1},{1,0},{2,3},{3,2},{4,5},{5,4},{6,7},{7,6},{8,9},{9,8},{10,11... | collective-permute-start | bytes 393224 | tf_op jit(solution)/shard_map/ppermute | solution.py:190
  23.3 4.8 %collective-permute-start.4 = (bf16[64,1024]{1,0:T(8,128)(2,1)S(1)}, bf16[64,1024]{1,0:T(8,128)(2,1)S(1)}, u32[]{:S(2)}, u32[]{:S(2)}) collective-permute-start(bf16[64,1024]{1,0:T(8,128)(2,1)S(1)} %collective-permute-done.3.refs_2_), channel_id=1, source_target_pairs={{0,1},{1,0},{2,3},{3,2},{4,5},{5,4},{6,7},{7,6},{8,9},{9,8},{10,11... | collective-permute-start | bytes 393224 | tf_op jit(solution)/shard_map/ppermute | solution.py:190
  23.7 4.3 %collective-permute-start.6 = (bf16[64,1024]{1,0:T(8,128)(2,1)S(1)}, bf16[64,1024]{1,0:T(8,128)(2,1)S(1)}, u32[]{:S(2)}, u32[]{:S(2)}) collective-permute-start(bf16[64,1024]{1,0:T(8,128)(2,1)S(1)} %collective-permute-done.5.refs_4_), channel_id=1, source_target_pairs={{0,1},{1,0},{2,3},{3,2},{4,5},{5,4},{6,7},{7,6},{8,9},{9,8},{10,11... | collective-permute-start | bytes 393224 | tf_op jit(solution)/shard_map/ppermute | solution.py:190
  23.8 4.3 %collective-permute-start.8 = (bf16[64,1024]{1,0:T(8,128)(2,1)S(1)}, bf16[64,1024]{1,0:T(8,128)(2,1)S(1)}, u32[]{:S(2)}, u32[]{:S(2)}) collective-permute-start(bf16[64,1024]{1,0:T(8,128)(2,1)S(1)} %collective-permute-done.7.refs_6_), channel_id=1, source_target_pairs={{0,1},{1,0},{2,3},{3,2},{4,5},{5,4},{6,7},{7,6},{8,9},{9,8},{10,11... | collective-permute-start | bytes 393224 | tf_op jit(solution)/shard_map/ppermute | solution.py:190
  24.3 1.9 %collective-permute-start.11 = (bf16[64,1152]{1,0:T(8,128)(2,1)S(1)}, bf16[64,1152]{1,0:T(8,128)(2,1)S(1)}, u32[]{:S(2)}, u32[]{:S(2)}) collective-permute-start(bf16[64,1152]{1,0:T(8,128)(2,1)S(1)} %collective-permute-done.10.mine_ref), channel_id=1, source_target_pairs={{0,1},{1,0},{2,3},{3,2},{4,5},{5,4},{6,7},{7,6},{8,9},{9,8},{10,11... | collective-permute-start | bytes 442376 | tf_op jit(solution)/shard_map/ppermute | solution.py:190
  28.0 30.2 %copy-start.1 = (f32[2,64,512]{2,1,0:T(8,128)S(1)}, f32[2,64,512]{2,1,0:T(8,128)}, u32[]{:S(2)}) copy-start(f32[2,64,512]{2,1,0:T(8,128)} %param.7) | copy-start | bytes 786436
  32.2 26.1 %all-to-all-start = ((bf16[16,2,64,256]{3,2,1,0:T(8,128)(2,1)}), bf16[16,2,64,256]{3,2,1,0:T(8,128)(2,1)S(1)}, u32[]{:S(2)}, u32[]{:S(2)}) async-start(bf16[16,2,64,256]{3,2,1,0:T(8,128)(2,1)} %bitcast.8), calls=%async_computation | async-start | bytes 2097152 | tf_op jit(solution)/shard_map/all_to_all | solution.py:221
where the time goes:
time: 59.7 us; the launch traced here: 59.1 us
  starting transfers between devices  23 us (39%)
  waiting for transfers between devices  22.1 us (37%)
  Pallas kernels  10.2 us (17%)
  local copies, waits for them, and re-layouts  1.88 us (3%)
  other arithmetic  1.71 us (3%)
    all_to_all x1, waiting for transfers between devices, shards(): received = lax.all_to_all(partial, OWNERS, 0, 0)  18.1 us
    ppermute x11, starting transfers between devices, turned(): lax.ppermute(value, axis, [(i, (i + distance) % size) for i in range(size)])  15.2 us
    all_to_all x1, starting transfers between devices, shards(): received = lax.all_to_all(partial, OWNERS, 0, 0)  7.15 us
    pallas_call x5, Pallas kernels, call(): pl.pallas_call(kernel, out_shape=out_shape, in_specs=specs or [VMEM] * le...  6.16 us
    pallas_call x1, Pallas kernels, correlate(): pl.pallas_call(correlate_kernel, grid=(2,), out_shape=jax.ShapeDtypeStruc...  4.08 us
    ppermute x11, waiting for transfers between devices, turned(): lax.ppermute(value, axis, [(i, (i + distance) % size) for i in range(size)])  3.98 us
    unnamed x6, local copies, waits for them, and re-layouts  1.64 us
  transfers between devices with their start and end apart: 13, of which 4 were waited for; matrix products, arithmetic and copies ran while one was open for 3% of the time, Pallas kernels for 7%

commit v1 on v0

v1 whole, which is shorter than its diff:
```python
import functools

import jax
import jax.numpy as jnp
from jax import lax
from jax.experimental import pallas as pl
from jax.experimental.pallas import tpu as pltpu
from jax.sharding import Mesh, PartitionSpec as P


CHAN = ("yh", "z")
TIME = ("x", "yl", "c")
OWNERS = ("yh", "x", "yl")
VMEM = pl.BlockSpec(memory_space=pltpu.VMEM)
NT = (((1,), (1,)), ((), ()))
TILE = 256
PAD = 128
MIB = 1 << 20


def call(kernel, out_shape, operands, mib, flops):
    return pl.pallas_call(
        kernel,
        out_shape=out_shape,
        in_specs=[VMEM] * len(operands),
        out_specs=jax.tree.map(lambda _: VMEM, out_shape),
        compiler_params=pltpu.CompilerParams(vmem_limit_bytes=mib * MIB),
        cost_estimate=pl.CostEstimate(flops=flops, bytes_accessed=MIB, transcendentals=0),
    )(*operands)


def edge_kernel(own_ref, edge_ref):
    width = edge_ref.shape[1]
    lower = lax.axis_index("c") == 0
    pl.when(lower)(lambda: pltpu.sync_copy(own_ref.at[:, :width], edge_ref))
    pl.when(jnp.logical_not(lower))(lambda: pltpu.sync_copy(own_ref.at[:, own_ref.shape[1] - width :], edge_ref))


def facing_edge(own, width):
    return pl.pallas_call(
        edge_kernel,
        out_shape=jax.ShapeDtypeStruct((own.shape[0], width), own.dtype),
        in_specs=[pl.BlockSpec(memory_space=pl.ANY)],
        out_specs=VMEM,
        compiler_params=pltpu.CompilerParams(vmem_limit_bytes=2 * MIB),
        name="edge",
    )(own)


def split(value):
    high = value.astype(jnp.bfloat16)
    return high, (value - high.astype(jnp.float32)).astype(jnp.bfloat16)


def prepare_kernel(taps_ref, own_ref, high_ref, low_ref, own_high_ref, own_low_ref):
    own_high_ref[...], own_low_ref[...] = split(own_ref[...])
    rows, width = high_ref.shape
    taps = taps_ref[...]
    row = jnp.concatenate([taps, jnp.zeros((1, width - taps.shape[1]), jnp.float32)], axis=1)
    matrix = pltpu.roll(jnp.broadcast_to(row, (rows, width)), 0, 1, stride=1, stride_axis=0)
    high_ref[...], low_ref[...] = split(matrix)


def prepare(whitening, own):
    matrix = jax.ShapeDtypeStruct((TILE, whitening.shape[0] + TILE), jnp.bfloat16)
    part = jax.ShapeDtypeStruct(own.shape, jnp.bfloat16)
    shapes = (matrix, matrix, part, part)
    return call(prepare_kernel, shapes, (whitening[None, :], own), 8, 10**9)


def filter_kernel(
    half_taps, beside_ref, across_ref, mat_high_ref, mat_low_ref, own_high_ref, own_low_ref, mine_ref, own_ref
):
    channels, seg_len = own_ref.shape
    width = mat_high_ref.shape[1]
    blocks = seg_len // TILE + 1
    lower = lax.axis_index("c") == 0
    reach = half_taps + PAD
    across = across_ref[...]
    low = split(jnp.where(lower, across, beside_ref[:, seg_len - reach :]))
    high = split(jnp.where(lower, beside_ref[:, :half_taps], across[:, :half_taps]))

    def stacked(before, own, after):
        zeros = jnp.zeros((channels, TILE - PAD), jnp.bfloat16)
        padded = jnp.concatenate([zeros, before, own, after], axis=1)
        return jnp.concatenate(
            [padded[:, b * TILE : b * TILE + width] for b in range(blocks)], axis=0
        )

    x_high = stacked(low[0], own_high_ref[...], high[0])
    x_low = stacked(low[1], own_low_ref[...], high[1])
    dot = functools.partial(lax.dot_general, dimension_numbers=NT, preferred_element_type=jnp.float32)
    total = dot(x_low, mat_high_ref[...]) + dot(x_high, mat_low_ref[...])
    total = total + dot(x_high, mat_high_ref[...])
    before = total[:channels, TILE - PAD :]
    before = jnp.where(lax.axis_index(TIME) == 0, jnp.zeros_like(before), before)
    mine_ref[:, :PAD] = before.astype(jnp.bfloat16)
    for b in range(1, blocks):
        piece = total[b * channels : (b + 1) * channels].astype(jnp.bfloat16)
        mine_ref[:, PAD + (b - 1) * TILE : PAD + b * TILE] = piece
        own_ref[:, (b - 1) * TILE : b * TILE] = piece


def filter_segment(beside, across, prepared, half_taps):
    channels, seg_len = beside.shape
    return call(
        functools.partial(filter_kernel, half_taps),
        (
            jax.ShapeDtypeStruct((channels, PAD + seg_len), jnp.bfloat16),
            jax.ShapeDtypeStruct((channels, seg_len), jnp.bfloat16),
        ),
        (beside, across, *prepared),
        12,
        10**9,
    )


def rows_kernel(lag_count, mine_ref, theirs_ref, rows_ref):
    channels, seg_len = mine_ref.shape[0], mine_ref.shape[1] - PAD
    core = lax.axis_index("c")
    mine, theirs = mine_ref[...], theirs_ref[...]
    first = jnp.where(core == 0, mine, theirs)
    second = jnp.where(core == 0, theirs, mine)
    both = jnp.concatenate([first, second[:, PAD:]], axis=1)
    both = jnp.where(core == 0, both, pltpu.roll(both, 2, 1))
    for index in range(lag_count):
        lag = 4 * (index // 2) + index % 2
        moved = both if lag == 0 else pltpu.roll(both, lag, 1)
        at = slice(index * channels, (index + 1) * channels)
        for k in range(2):
            begin = pl.multiple_of((core if k == 0 else 1 - core) * seg_len, seg_len)
            rows_ref[at, pl.ds(begin, seg_len)] = moved[:, PAD + k * seg_len : PAD + (k + 1) * seg_len]


def lagged_rows(mine, theirs, lag_count):
    channels, width = mine.shape
    return call(
        functools.partial(rows_kernel, lag_count),
        jax.ShapeDtypeStruct((lag_count * channels, 2 * (width - PAD)), jnp.bfloat16),
        (mine, theirs),
        8,
        2 * 10**9,
    )


def correlate_kernel(*refs):
    *piece_refs, mine_ref, other_ref, out_ref = refs
    split_at = len(piece_refs) - 2
    seg_len = piece_refs[0].shape[1]
    side = pl.program_id(0)

    def fill(rows_ref):
        total = 0.0
        for k in range(2):
            refs = piece_refs[split_at:] if k else piece_refs[:split_at]
            cols = jnp.concatenate([ref[:, ref.shape[1] - seg_len :] for ref in refs], axis=0)
            rows = rows_ref[:, k * seg_len : (k + 1) * seg_len]
            total = total + lax.dot_general(rows, cols, NT, preferred_element_type=jnp.float32)
        out_ref[0] = total.astype(jnp.bfloat16)

    pl.when(side == lax.axis_index("yh"))(lambda: fill(mine_ref))
    pl.when(side != lax.axis_index("yh"))(lambda: fill(other_ref))


def correlate(pieces, mine_rows, other_rows):
    width = pieces[0].shape[0] * (len(pieces) - 2)
    rows = mine_rows.shape[0]
    return pl.pallas_call(
        correlate_kernel,
        grid=(2,),
        out_shape=jax.ShapeDtypeStruct((2, rows, width), jnp.bfloat16),
        in_specs=[VMEM] * (len(pieces) + 2),
        out_specs=pl.BlockSpec((1, rows, width), lambda side: (side, 0, 0)),
        compiler_params=pltpu.CompilerParams(vmem_limit_bytes=6 * MIB),
        cost_estimate=pl.CostEstimate(flops=4 * 10**9, bytes_accessed=MIB, transcendentals=0),
        name="correlate",
    )(*pieces, mine_rows, other_rows)


def stack_kernel(parts_ref, weights_ref, old_ref, out_ref):
    count, width = parts_ref.shape[1], parts_ref.shape[-1]
    for side in range(2):
        at = slice(side * width, (side + 1) * width)
        total = parts_ref[side, 0].astype(jnp.float32)
        for k in range(1, count):
            total = total + parts_ref[side, k].astype(jnp.float32)
        total = pltpu.roll(total, lax.axis_index("z") * parts_ref.shape[2] // 2, 1)
        out_ref[:, at] = old_ref[:, at] + total * weights_ref[:, at]


def stack(parts, weights, old_stack):
    lags, channels, width = old_stack.shape
    parts = parts.reshape(2, -1, lags * channels, parts.shape[-1])
    shape = jax.ShapeDtypeStruct((lags * channels, width), jnp.float32)
    old = old_stack.reshape(lags * channels, width)
    return call(stack_kernel, shape, (parts, weights, old), 8, 10**8).reshape(old_stack.shape)


def turned(value, axis, distance):
    size = lax.axis_size(axis)
    return lax.ppermute(value, axis, [(i, (i + distance) % size) for i in range(size)])


def shards(raw_strain, whitening, block_mask, old_stack):
    channels, seg_len = raw_strain.shape
    half_taps = whitening.shape[0] // 2
    segments = lax.axis_size(TIME)
    lags = old_stack.shape[0]
    z, yh, zs = lax.axis_index("z"), lax.axis_index("yh"), lax.axis_size("z")
    reach = half_taps + PAD
    edge = facing_edge(raw_strain, reach)
    pairs = [(i, i + 1) for i in range(1, segments - 1, 2)]
    across = lax.ppermute(edge, TIME, pairs + [(b, a) for a, b in pairs])
    beside = turned(raw_strain, "c", 1)
    prepared = prepare(whitening, raw_strain)
    mine, own = filter_segment(beside, across, prepared, half_taps)
    other = turned(mine, "yh", 1)
    pieces = []
    for d in range(zs):
        piece = turned(own, "z", (zs - d) % zs) if d else own
        pieces.append(piece)
    mine_swapped = turned(mine, "c", 1)
    pieces += [mine_swapped, turned(jnp.concatenate(pieces[1:], axis=0), "c", 1)]
    lag_count = lags * segments // 2
    other_swapped = turned(other, "c", 1)
    mine_rows = lagged_rows(mine, mine_swapped, lag_count)
    other_rows = lagged_rows(other, other_swapped, lag_count)
    partial = correlate(pieces, mine_rows, other_rows)
    partial = partial.reshape(segments, lags, channels, -1)
    received = lax.all_to_all(partial, OWNERS, 0, 0)
    scaling = float(seg_len * segments) ** (-0.5)
    weights = jnp.repeat(block_mask[yh * zs + z].astype(jnp.float32) * scaling, channels)[None, :]
    return stack(received, weights, old_stack)


def solution(mesh):
    fine = Mesh(mesh.devices.reshape(2, 4, 4, 2, 2), CHAN + TIME)
    in_specs = (P(CHAN, TIME), P(), P(), P(TIME, CHAN, None))
    out_specs = P(TIME, CHAN, None)
    return jax.shard_map(shards, mesh=fine, in_specs=in_specs, out_specs=out_specs, check_vma=False)
```

time: 59.7 us -> 57.5 us (0.963)
  starting transfers between devices: 23 us -> 27.9 us
  waiting for transfers between devices: 22.1 us -> 17.7 us
  Pallas kernels: 10.2 us -> 8.06 us
  other arithmetic: 1.71 us -> 0.73 us
  local copies, waits for them, and re-layouts: 1.88 us -> 2.74 us
    all_to_all x1, starting transfers between devices: 7.15 us -> 11.9 us  [shards(): received = lax.all_to_all(partial, OWNERS, 0, 0)]
    ppermute x11 -> x8, waiting for transfers between devices: 3.98 us -> 0.17 us  [turned(): lax.ppermute(value, axis, [(i, (i + distance) % size) for i in range(size)])]
    pallas_call x5 -> x6, Pallas kernels: 6.16 us -> 4.62 us  [the longest x5 4.6 us: call(): pl.pallas_call(kernel, out_shape=out_shape, in_specs=[VMEM] * len(operand...]
    select_n x1 -> x0, other arithmetic: 1.01 us -> none  [shards(): jnp.where(core == 0, raw_strain[:, :reach], raw_strain[:, seg_len - reach:])]
    unnamed x6 -> x8, local copies, waits for them, and re-layouts: 1.64 us -> 2.59 us
    pallas_call x1, Pallas kernels: 4.08 us -> 3.44 us  [correlate(): pl.pallas_call(correlate_kernel, grid=(2,), out_shape=jax.ShapeDtypeStruc...]
    ppermute x11 -> x8, starting transfers between devices: 15.2 us -> 15.3 us  [turned(): lax.ppermute(value, axis, [(i, (i + distance) % size) for i in range(size)])]
  transfers between devices with their start and end apart: 13 -> 10, of which waited for: 4 -> 2; matrix products, arithmetic and copies ran while one was open for 3% -> 2% of each run, Pallas kernels for 7% -> 5%
where the time goes in v1:
time: 57.5 us; the launch traced here: 57.2 us
  starting transfers between devices  27.9 us (49%)
  waiting for transfers between devices  17.7 us (31%)
  Pallas kernels  8.06 us (14%)
  local copies, waits for them, and re-layouts  2.74 us (5%)
  other arithmetic  0.73 us (1%)
    all_to_all x1, waiting for transfers between devices, shards(): received = lax.all_to_all(partial, OWNERS, 0, 0)  17.5 us
    ppermute x8, starting transfers between devices, turned(): lax.ppermute(value, axis, [(i, (i + distance) % size) for i in range(size)])  15.3 us
    all_to_all x1, starting transfers between devices, shards(): received = lax.all_to_all(partial, OWNERS, 0, 0)  11.9 us
    pallas_call x5, Pallas kernels, call(): pl.pallas_call(kernel, out_shape=out_shape, in_specs=[VMEM] * len(operand...  4.6 us
    pallas_call x1, Pallas kernels, correlate(): pl.pallas_call(correlate_kernel, grid=(2,), out_shape=jax.ShapeDtypeStruc...  3.44 us
    unnamed x8, local copies, waits for them, and re-layouts  2.59 us
  transfers between devices with their start and end apart: 10, of which 2 were waited for; matrix products, arithmetic and copies ran while one was open for 2% of the time, Pallas kernels for 5%

profile of v1, /device:TPU:0, one launch (start us, length us, event | category | flops | bytes accessed | tf_op | source)
XLA Modules:
  0.0 57.2 jit_solution(5516214961434218752)
XLA Ops:
  0.0 0.9 %copy-done = f32[64,1024]{1,0:T(8,128)S(1)} copy-done((f32[64,1024]{1,0:T(8,128)S(1)}, f32[64,1024]{1,0:T(8,128)}, u32[]{:S(2)}) %copy-start) | copy-done | bytes 262168
  1.0 0.7 %collective-permute-start.1 = (f32[64,640]{1,0:T(8,128)S(1)}, f32[64,640]{1,0:T(8,128)S(1)}, u32[]{:S(2)}, u32[]{:S(2)}) collective-permute-start(f32[64,640]{1,0:T(8,128)S(1)} %edge.1), channel_id=1, source_target_pairs={{1,2},{3,4},{5,6},{7,8},{9,10},{11,12},{13,14},{2,1},{4,3},{6,5},{... | collective-permute-start | bytes 491528 | tf_op jit(solution)/shard_map/ppermute | solution.py:213
  1.7 0.0 copy-start.1
  1.7 0.9 %copy-done.1 = f32[64,1024]{1,0:T(8,128)S(1)} copy-done((f32[64,1024]{1,0:T(8,128)S(1)}, f32[64,1024]{1,0:T(8,128)}, u32[]{:S(2)}) %copy-start.1) | copy-done | bytes 262168
  2.6 0.7 %copy-done.3 = f32[1024]{0:T(1024)S(1)} copy-done((f32[1024]{0:T(1024)S(1)}, f32[1024]{0:T(1024)}, u32[]{:S(2)}) %copy-start.3) | copy-done | bytes 4120
  3.3 0.3 shard_map.46
  3.6 0.8 %shard_map.47 = (bf16[64,1152]{1,0:T(8,128)(2,1)S(1)}, bf16[64,1024]{1,0:T(8,128)(2,1)S(1)}) custom-call(f32[64,1024]{1,0:T(8,128)S(1)} %collective-permute-done.beside_ref, f32[64,640]{1,0:T(8,128)S(1)} %collective-permute-done.1.across_ref, bf16[256,1280]{1,0:T(8,128)(2,1)S(1)} %get-tuple-element.11.mat_high_ref, ...), custom_call_target="tpu_custom_call" | custom-call | flops 1000000000 | bytes 1048576 | tf_op jit(solution)/shard_map/pallas_call | solution.py:22
  4.4 4.2 %collective-permute-start.2 = (bf16[64,1024]{1,0:T(8,128)(2,1)S(1)}, bf16[64,1024]{1,0:T(8,128)(2,1)S(1)}, u32[]{:S(2)}, u32[]{:S(2)}) collective-permute-start(bf16[64,1024]{1,0:T(8,128)(2,1)S(1)} %get-tuple-element.15.refs_0_), channel_id=1, source_target_pairs={{0,48},{16,0},{32,16},{48,32},{1,49},{17,1},{33,17},{49,33},{2,50}... | collective-permute-start | bytes 393224 | tf_op jit(solution)/shard_map/ppermute | solution.py:201
  8.7 1.3 %collective-permute-start.4 = (bf16[64,1024]{1,0:T(8,128)(2,1)S(1)}, bf16[64,1024]{1,0:T(8,128)(2,1)S(1)}, u32[]{:S(2)}, u32[]{:S(2)}) collective-permute-start(bf16[64,1024]{1,0:T(8,128)(2,1)S(1)} %get-tuple-element.15.refs_0_), channel_id=1, source_target_pairs={{0,16},{16,32},{32,48},{48,0},{1,17},{17,33},{33,49},{49,1},{2,18}... | collective-permute-start | bytes 393224 | tf_op jit(solution)/shard_map/ppermute | solution.py:201
  9.9 3.2 %collective-permute-start.7 = (bf16[64,1152]{1,0:T(8,128)(2,1)S(1)}, bf16[64,1152]{1,0:T(8,128)(2,1)S(1)}, u32[]{:S(2)}, u32[]{:S(2)}) collective-permute-start(bf16[64,1152]{1,0:T(8,128)(2,1)S(1)} %get-tuple-element.16.mine_ref), channel_id=1, source_target_pairs={{0,64},{64,0},{1,65},{65,1},{2,66},{66,2},{3,67},{67,3},{4,68},{68... | collective-permute-start | bytes 442376 | tf_op jit(solution)/shard_map/ppermute | solution.py:201
  13.1 3.7 %collective-permute-start.5 = (bf16[64,1152]{1,0:T(8,128)(2,1)S(1)}, bf16[64,1152]{1,0:T(8,128)(2,1)S(1)}, u32[]{:S(2)}, u32[]{:S(2)}) collective-permute-start(bf16[64,1152]{1,0:T(8,128)(2,1)S(1)} %get-tuple-element.16.mine_ref), channel_id=1, source_target_pairs={{0,1},{1,0},{2,3},{3,2},{4,5},{5,4},{6,7},{7,6},{8,9},{9,8},{10,11... | collective-permute-start | bytes 442376 | tf_op jit(solution)/shard_map/ppermute | solution.py:201
  16.9 2.8 %collective-permute-start.6 = (bf16[192,1024]{1,0:T(8,128)(2,1)S(1)}, bf16[192,1024]{1,0:T(8,128)(2,1)S(1)}, u32[]{:S(2)}, u32[]{:S(2)}) collective-permute-start(bf16[192,1024]{1,0:T(8,128)(2,1)S(1)} %pad_maximum_fusion), channel_id=1, source_target_pairs={{0,1},{1,0},{2,3},{3,2},{4,5},{5,4},{6,7},{7,6},{8,9},{9,8},{10,11... | collective-permute-start | bytes 1179656 | tf_op jit(solution)/shard_map/ppermute | solution.py:201
  19.7 0.1 collective-permute-start.8
  19.8 1.3 %shard_map.48.refs_6_ = bf16[1024,2048]{1,0:T(8,128)(2,1)S(1)} custom-call(bf16[64,1152]{1,0:T(8,128)(2,1)S(1)} %get-tuple-element.16.mine_ref, bf16[64,1152]{1,0:T(8,128)(2,1)S(1)} %collective-permute-done.5.theirs_ref.refs_4_), custom_call_target="tpu_custom_call" | custom-call | flops 2000000000 | bytes 1048576 | tf_op jit(solution)/shard_map/pallas_call | solution.py:22
  21.1 0.2 collective-permute-done.8.theirs_ref
  21.2 1.3 %shard_map.49.refs_7_ = bf16[1024,2048]{1,0:T(8,128)(2,1)S(1)} custom-call(bf16[64,1152]{1,0:T(8,128)(2,1)S(1)} %collective-permute-done.7.mine_ref, bf16[64,1152]{1,0:T(8,128)(2,1)S(1)} %collective-permute-done.8.theirs_ref), custom_call_target="tpu_custom_call" | custom-call | flops 2000000000 | bytes 1048576 | tf_op jit(solution)/shard_map/pallas_call | solution.py:22
  22.5 0.0 copy-start.2
  22.6 3.4 %correlate.1 = bf16[2,1024,256]{2,1,0:T(8,128)(2,1)} custom-call(bf16[64,1024]{1,0:T(8,128)(2,1)S(1)} %get-tuple-element.15.refs_0_, bf16[64,1024]{1,0:T(8,128)(2,1)S(1)} %collective-permute-done.2.refs_1_, bf16[64,1024]{1,0:T(8,128)(2,1)S(1)} %collective-permute-done.3.refs_2_, bf16[64,1024]{1,0:T(8,128)(2,1)S(1)} %collective-permute-done.4.refs_3_, ...), custom_call_target="tpu_custom_call" | custom-call | flops 4000000000 | bytes 1048576 | tf_op jit(solution)/shard_map/correlate/pallas_call | solution.py:168
  26.0 11.9 %all-to-all-start = ((bf16[16,2,64,256]{3,2,1,0:T(8,128)(2,1)}), bf16[16,2,64,256]{3,2,1,0:T(8,128)(2,1)S(1)}, u32[]{:S(2)}, u32[]{:S(2)}) async-start(bf16[16,2,64,256]{3,2,1,0:T(8,128)(2,1)} %bitcast.1), calls=%async_computation | async-start | bytes 2097152 | tf_op jit(solution)/shard_map/all_to_all | solution.py:230
  37.9 0.7 %multiply_bitcast_fusion = f32[8]{0:T(128)S(1)} fusion(s32[8,8]{1,0:T(8,128)} %param.6, s32[]{:T(128)S(6)} %select_n.3), kind=kLoop, calls=%fused_computation.1 | loop fusion | flops 16 | bytes 68 | tf_op jit(solution)/shard_map/mul | solution.py:232
  38.6 0.1 broadcast_in_dim.7
  38.7 0.1 broadcast_in_dim_reshape.3.weights_ref
  38.8 17.5 %all-to-all-done = bf16[16,2,64,256]{3,2,1,0:T(8,128)(2,1)S(1)} async-done(((bf16[16,2,64,256]{3,2,1,0:T(8,128)(2,1)}), bf16[16,2,64,256]{3,2,1,0:T(8,128)(2,1)S(1)}, u32[]{:S(2)}, u32[]{:S(2)}) %all-to-all-start) | async-done | bytes 1048608 | tf_op jit(solution)/shard_map/all_to_all | solution.py:230
  56.3 0.9 %shard_map.50 = f32[128,512]{1,0:T(8,128)} custom-call(bf16[2,8,128,256]{3,2,1,0:T(8,128)(2,1)S(1)} %bitcast.7, f32[1,512]{1,0:T(1,128)S(1)} %broadcast_in_dim_reshape.3.weights_ref, f32[128,512]{1,0:T(8,128)S(1)} %bitcast.8), custom_call_target="tpu_custom_call" | custom-call | flops 100000000 | bytes 1048576 | tf_op jit(solution)/shard_map/pallas_call | solution.py:22
  (15 shorter events, 0.1 us)
Async XLA Ops:
  0.0 3.6 %collective-permute-start = (f32[64,1024]{1,0:T(8,128)}, f32[64,1024]{1,0:T(8,128)S(1)}, u32[]{:S(2)}, u32[]{:S(2)}) collective-permute-start(f32[64,1024]{1,0:T(8,128)} %own_ref.3), channel_id=1, source_target_pairs={{0,1},{1,0},{2,3},{3,2},{4,5},{5,4},{6,7},{7,6},{8,9},{9,8},{10,11... | collective-permute-start | bytes 786440 | tf_op jit(solution)/shard_map/ppermute | solution.py:201
  0.0 1.0 %copy-start = (f32[64,1024]{1,0:T(8,128)S(1)}, f32[64,1024]{1,0:T(8,128)}, u32[]{:S(2)}) copy-start(f32[64,1024]{1,0:T(8,128)} %own_ref.3) | copy-start | bytes 786436
  1.0 2.6 %collective-permute-start.1 = (f32[64,640]{1,0:T(8,128)S(1)}, f32[64,640]{1,0:T(8,128)S(1)}, u32[]{:S(2)}, u32[]{:S(2)}) collective-permute-start(f32[64,640]{1,0:T(8,128)S(1)} %edge.1), channel_id=1, source_target_pairs={{1,2},{3,4},{5,6},{7,8},{9,10},{11,12},{13,14},{2,1},{4,3},{6,5},{... | collective-permute-start | bytes 491528 | tf_op jit(solution)/shard_map/ppermute | solution.py:213
  1.7 1.0 %copy-start.1 = (f32[64,1024]{1,0:T(8,128)S(1)}, f32[64,1024]{1,0:T(8,128)}, u32[]{:S(2)}) copy-start(f32[64,1024]{1,0:T(8,128)} %own_ref.3) | copy-start | bytes 786436
  2.6 0.7 %copy-start.3 = (f32[1024]{0:T(1024)S(1)}, f32[1024]{0:T(1024)}, u32[]{:S(2)}) copy-start(f32[1024]{0:T(1024)} %param.5) | copy-start | bytes 12292
  4.4 12.4 %collective-permute-start.2 = (bf16[64,1024]{1,0:T(8,128)(2,1)S(1)}, bf16[64,1024]{1,0:T(8,128)(2,1)S(1)}, u32[]{:S(2)}, u32[]{:S(2)}) collective-permute-start(bf16[64,1024]{1,0:T(8,128)(2,1)S(1)} %get-tuple-element.15.refs_0_), channel_id=1, source_target_pairs={{0,48},{16,0},{32,16},{48,32},{1,49},{17,1},{33,17},{49,33},{2,50}... | collective-permute-start | bytes 393224 | tf_op jit(solution)/shard_map/ppermute | solution.py:201
  8.7 8.2 %collective-permute-start.3 = (bf16[64,1024]{1,0:T(8,128)(2,1)S(1)}, bf16[64,1024]{1,0:T(8,128)(2,1)S(1)}, u32[]{:S(2)}, u32[]{:S(2)}) collective-permute-start(bf16[64,1024]{1,0:T(8,128)(2,1)S(1)} %get-tuple-element.15.refs_0_), channel_id=1, source_target_pairs={{0,32},{16,48},{32,0},{48,16},{1,33},{17,49},{33,1},{49,17},{2,34}... | collective-permute-start | bytes 393224 | tf_op jit(solution)/shard_map/ppermute | solution.py:201
  8.7 8.2 %collective-permute-start.4 = (bf16[64,1024]{1,0:T(8,128)(2,1)S(1)}, bf16[64,1024]{1,0:T(8,128)(2,1)S(1)}, u32[]{:S(2)}, u32[]{:S(2)}) collective-permute-start(bf16[64,1024]{1,0:T(8,128)(2,1)S(1)} %get-tuple-element.15.refs_0_), channel_id=1, source_target_pairs={{0,16},{16,32},{32,48},{48,0},{1,17},{17,33},{33,49},{49,1},{2,18}... | collective-permute-start | bytes 393224 | tf_op jit(solution)/shard_map/ppermute | solution.py:201
  9.9 9.8 %collective-permute-start.7 = (bf16[64,1152]{1,0:T(8,128)(2,1)S(1)}, bf16[64,1152]{1,0:T(8,128)(2,1)S(1)}, u32[]{:S(2)}, u32[]{:S(2)}) collective-permute-start(bf16[64,1152]{1,0:T(8,128)(2,1)S(1)} %get-tuple-element.16.mine_ref), channel_id=1, source_target_pairs={{0,64},{64,0},{1,65},{65,1},{2,66},{66,2},{3,67},{67,3},{4,68},{68... | collective-permute-start | bytes 442376 | tf_op jit(solution)/shard_map/ppermute | solution.py:201
  13.1 6.7 %collective-permute-start.5 = (bf16[64,1152]{1,0:T(8,128)(2,1)S(1)}, bf16[64,1152]{1,0:T(8,128)(2,1)S(1)}, u32[]{:S(2)}, u32[]{:S(2)}) collective-permute-start(bf16[64,1152]{1,0:T(8,128)(2,1)S(1)} %get-tuple-element.16.mine_ref), channel_id=1, source_target_pairs={{0,1},{1,0},{2,3},{3,2},{4,5},{5,4},{6,7},{7,6},{8,9},{9,8},{10,11... | collective-permute-start | bytes 442376 | tf_op jit(solution)/shard_map/ppermute | solution.py:201
  16.9 5.7 %collective-permute-start.6 = (bf16[192,1024]{1,0:T(8,128)(2,1)S(1)}, bf16[192,1024]{1,0:T(8,128)(2,1)S(1)}, u32[]{:S(2)}, u32[]{:S(2)}) collective-permute-start(bf16[192,1024]{1,0:T(8,128)(2,1)S(1)} %pad_maximum_fusion), channel_id=1, source_target_pairs={{0,1},{1,0},{2,3},{3,2},{4,5},{5,4},{6,7},{7,6},{8,9},{9,8},{10,11... | collective-permute-start | bytes 1179656 | tf_op jit(solution)/shard_map/ppermute | solution.py:201
  19.7 1.6 %collective-permute-start.8 = (bf16[64,1152]{1,0:T(8,128)(2,1)S(1)}, bf16[64,1152]{1,0:T(8,128)(2,1)S(1)}, u32[]{:S(2)}, u32[]{:S(2)}) collective-permute-start(bf16[64,1152]{1,0:T(8,128)(2,1)S(1)} %collective-permute-done.7.mine_ref), channel_id=1, source_target_pairs={{0,1},{1,0},{2,3},{3,2},{4,5},{5,4},{6,7},{7,6},{8,9},{9,8},{10,11... | collective-permute-start | bytes 442376 | tf_op jit(solution)/shard_map/ppermute | solution.py:201
  22.5 33.7 %copy-start.2 = (f32[2,64,512]{2,1,0:T(8,128)S(1)}, f32[2,64,512]{2,1,0:T(8,128)}, u32[]{:S(2)}) copy-start(f32[2,64,512]{2,1,0:T(8,128)} %param.7) | copy-start | bytes 786436
  26.0 30.3 %all-to-all-start = ((bf16[16,2,64,256]{3,2,1,0:T(8,128)(2,1)}), bf16[16,2,64,256]{3,2,1,0:T(8,128)(2,1)S(1)}, u32[]{:S(2)}, u32[]{:S(2)}) async-start(bf16[16,2,64,256]{3,2,1,0:T(8,128)(2,1)} %bitcast.1), calls=%async_computation | async-start | bytes 2097152 | tf_op jit(solution)/shard_map/all_to_all | solution.py:230

commit v2 on v1

--- a/solution.py
+++ b/solution.py
@@ -10,7 +10,6 @@
 
 CHAN = ("yh", "z")
 TIME = ("x", "yl", "c")
-OWNERS = ("yh", "x", "yl")
 VMEM = pl.BlockSpec(memory_space=pltpu.VMEM)
 NT = (((1,), (1,)), ((), ()))
 TILE = 256
@@ -124,9 +123,12 @@
     both = jnp.concatenate([first, second[:, PAD:]], axis=1)
     both = jnp.where(core == 0, both, pltpu.roll(both, 2, 1))
     for index in range(lag_count):
-        lag = 4 * (index // 2) + index % 2
+        group, second = index // 2, index % 2
+        lag = 4 * group + second
         moved = both if lag == 0 else pltpu.roll(both, lag, 1)
-        at = slice(index * channels, (index + 1) * channels)
+        groups = lag_count // 2
+        place = jnp.where(core == 0, group, group % 2 * (groups // 2) + group // 2)
+        at = pl.ds(pl.multiple_of((2 * place + second) * channels, channels), channels)
         for k in range(2):
             begin = pl.multiple_of((core if k == 0 else 1 - core) * seg_len, seg_len)
             rows_ref[at, pl.ds(begin, seg_len)] = moved[:, PAD + k * seg_len : PAD + (k + 1) * seg_len]
@@ -143,57 +145,133 @@
     )
 
 
-def correlate_kernel(*refs):
+def position():
+    core, x, y = lax.axis_index("c"), lax.axis_index("x"), 2 * lax.axis_index("yh") + lax.axis_index("yl")
+    return core, x, y
+
+
+def chunk_kernel(distance, *refs):
     *piece_refs, mine_ref, other_ref, out_ref = refs
-    split_at = len(piece_refs) - 2
     seg_len = piece_refs[0].shape[1]
-    side = pl.program_id(0)
-
-    def fill(rows_ref):
+    rows = out_ref.shape[0] // 2
+    core, x, y = position()
+    yh = lax.axis_index("yh")
+    to_x, to_y = lax.rem(x + distance, 4), lax.rem(y + distance, 4)
+
+    def fill(first_ref, second_ref, first_at, second_at):
         total = 0.0
         for k in range(2):
-            refs = piece_refs[split_at:] if k else piece_refs[:split_at]
+            refs = piece_refs[-2:] if k else piece_refs[:-2]
             cols = jnp.concatenate([ref[:, ref.shape[1] - seg_len :] for ref in refs], axis=0)
-            rows = rows_ref[:, k * seg_len : (k + 1) * seg_len]
-            total = total + lax.dot_general(rows, cols, NT, preferred_element_type=jnp.float32)
-        out_ref[0] = total.astype(jnp.bfloat16)
-
-    pl.when(side == lax.axis_index("yh"))(lambda: fill(mine_ref))
-    pl.when(side != lax.axis_index("yh"))(lambda: fill(other_ref))
-
-
-def correlate(pieces, mine_rows, other_rows):
+            part = slice(k * seg_len, (k + 1) * seg_len)
+            left = jnp.concatenate(
+                [
+                    ref[pl.ds(pl.multiple_of(at, rows), rows), part]
+                    for ref, at in ((first_ref, first_at), (second_ref, second_at))
+                ],
+                axis=0,
+            )
+            total = total + lax.dot_general(left, cols, NT, preferred_element_type=jnp.float32)
+        out_ref[...] = total.astype(out_ref.dtype)
+
+    along_x = to_x * rows
+    along_y = lax.rem(to_y, 2) * 2 * rows
+    stays = to_y // 2 == yh
+    is_x = core == 0
+
+    @pl.when(is_x & (yh == 0))
+    def _():
+        fill(mine_ref, other_ref, along_x, along_x)
+
+    @pl.when(is_x & (yh != 0))
+    def _():
+        fill(other_ref, mine_ref, along_x, along_x)
+
+    @pl.when(jnp.logical_not(is_x) & stays)
+    def _():
+        fill(mine_ref, mine_ref, along_y, along_y + rows)
+
+    @pl.when(jnp.logical_not(is_x) & jnp.logical_not(stays))
+    def _():
+        fill(other_ref, other_ref, along_y, along_y + rows)
+
+
+def chunk(pieces, mine_rows, other_rows, distance):
     width = pieces[0].shape[0] * (len(pieces) - 2)
-    rows = mine_rows.shape[0]
-    return pl.pallas_call(
-        correlate_kernel,
-        grid=(2,),
-        out_shape=jax.ShapeDtypeStruct((2, rows, width), jnp.bfloat16),
-        in_specs=[VMEM] * (len(pieces) + 2),
-        out_specs=pl.BlockSpec((1, rows, width), lambda side: (side, 0, 0)),
-        compiler_params=pltpu.CompilerParams(vmem_limit_bytes=6 * MIB),
-        cost_estimate=pl.CostEstimate(flops=4 * 10**9, bytes_accessed=MIB, transcendentals=0),
-        name="correlate",
-    )(*pieces, mine_rows, other_rows)
-
-
-def stack_kernel(parts_ref, weights_ref, old_ref, out_ref):
-    count, width = parts_ref.shape[1], parts_ref.shape[-1]
-    for side in range(2):
-        at = slice(side * width, (side + 1) * width)
-        total = parts_ref[side, 0].astype(jnp.float32)
-        for k in range(1, count):
-            total = total + parts_ref[side, k].astype(jnp.float32)
-        total = pltpu.roll(total, lax.axis_index("z") * parts_ref.shape[2] // 2, 1)
+    kind = jnp.bfloat16 if distance else jnp.float32
+    return call(
+        functools.partial(chunk_kernel, distance),
+        jax.ShapeDtypeStruct((mine_rows.shape[0] // 2, width), kind),
+        (*pieces, mine_rows, other_rows),
+        6,
+        10**9,
+    )
+
+
+def by_column_half(own, first, second, third):
+    last = lax.axis_index("yl") == 0
+    near, far = jnp.where(last, third, first), jnp.where(last, first, third)
+    return own + near, second + far
+
+
+def middle_kernel(own_ref, first_ref, second_ref, third_ref, own_out_ref, *out_refs):
+    rows = own_out_ref.shape[1]
+    core, x, y = position()
+    base = jnp.where(core == 0, y, x)
+    for distance, out_ref in enumerate((own_out_ref, *out_refs)):
+        at = pl.ds(pl.multiple_of(lax.rem(base + distance, 4) * rows, rows), rows)
+        own = own_ref[at, :]
+        parts = [ref[at, :].astype(jnp.float32) for ref in (first_ref, second_ref, third_ref)]
+        total = own + parts[0] + parts[1] + parts[2]
+        same, cross = by_column_half(own, *parts)
+        if distance == 0:
+            out_ref[0] = jnp.where(core == 0, total, same)
+            out_ref[1] = jnp.where(core == 0, jnp.zeros_like(total), cross)
+        else:
+            rounded = total.astype(jnp.bfloat16).astype(jnp.float32)
+            out_ref[0] = jnp.where(core == 0, rounded, same).astype(jnp.bfloat16)
+            out_ref[1] = jnp.where(core == 0, total - rounded, cross).astype(jnp.bfloat16)
+
+
+def middle(own, first, second, third):
+    rows, width = own.shape
+    shape = (2, rows // 4, width)
+    shapes = (jax.ShapeDtypeStruct(shape, jnp.float32),) + (jax.ShapeDtypeStruct(shape, jnp.bfloat16),) * 3
+    return call(middle_kernel, shapes, (own, first, second, third), 8, 10**9)
+
+
+def stack_kernel(own_ref, first_ref, second_ref, third_ref, weights_ref, old_ref, out_ref):
+    width = own_ref.shape[-1]
+    core, _, _ = position()
+    yh = lax.axis_index("yh")
+    pairs = [[ref[h].astype(jnp.float32) for h in range(2)] for ref in (first_ref, second_ref, third_ref)]
+    x_last = [own_ref[h] + pairs[0][h] + pairs[1][h] + pairs[2][h] for h in range(2)]
+    y_last = by_column_half(own_ref[0], *[a + b for a, b in pairs])
+    turn = lax.axis_index("z") * (out_ref.shape[0] // 2)
+    for h in range(2):
+        total = pltpu.roll(jnp.where(core == 0, y_last[h], x_last[h]), turn, 1)
+        half = yh if h == 0 else 1 - yh
+        at = pl.ds(pl.multiple_of(half * width, width), width)
         out_ref[:, at] = old_ref[:, at] + total * weights_ref[:, at]
 
 
 def stack(parts, weights, old_stack):
     lags, channels, width = old_stack.shape
-    parts = parts.reshape(2, -1, lags * channels, parts.shape[-1])
     shape = jax.ShapeDtypeStruct((lags * channels, width), jnp.float32)
     old = old_stack.reshape(lags * channels, width)
-    return call(stack_kernel, shape, (parts, weights, old), 8, 10**8).reshape(old_stack.shape)
+    return call(stack_kernel, shape, (*parts, weights, old), 8, 10**8).reshape(old_stack.shape)
+
+
+def passed(value, distance, x_core):
+    axes = ("yh", "x", "yl", "c")
+    pairs = []
+    for x in range(4):
+        for y in range(4):
+            for core in range(2):
+                to_x, to_y = ((x + distance) % 4, y) if core == x_core else (x, (y + distance) % 4)
+                source, target = (((b // 2 * 4 + a) * 2 + b % 2) * 2 + core for a, b in ((x, y), (to_x, to_y)))
+                pairs.append((source, target))
+    return lax.ppermute(value, axes, pairs)
 
 
 def turned(value, axis, distance):
@@ -225,12 +303,16 @@
     other_swapped = turned(other, "c", 1)
     mine_rows = lagged_rows(mine, mine_swapped, lag_count)
     other_rows = lagged_rows(other, other_swapped, lag_count)
-    partial = correlate(pieces, mine_rows, other_rows)
-    partial = partial.reshape(segments, lags, channels, -1)
-    received = lax.all_to_all(partial, OWNERS, 0, 0)
+    sums = {}
+    for d in (2, 1, 3, 0):
+        sums[d] = chunk(pieces, mine_rows, other_rows, d)
+        if d:
+            sums[d] = passed(sums[d], d, 0)
+    own_part, *parts = middle(*[sums[d] for d in range(4)])
+    parts = [own_part] + [passed(part, d, 1) for d, part in enumerate(parts, 1)]
     scaling = float(seg_len * segments) ** (-0.5)
     weights = jnp.repeat(block_mask[yh * zs + z].astype(jnp.float32) * scaling, channels)[None, :]
-    return stack(received, weights, old_stack)
+    return stack(parts, weights, old_stack)
 
 
 def solution(mesh):

time: 57.5 us -> 52.9 us (0.920)
  waiting for transfers between devices: 17.7 us -> 9.13 us
  starting transfers between devices: 27.9 us -> 31.4 us
    all_to_all x1 -> x0, waiting for transfers between devices: 17.5 us -> none  [shards(): received = lax.all_to_all(partial, OWNERS, 0, 0)]
    ppermute x0 -> x6, starting transfers between devices: none -> 15.4 us  [passed(): return lax.ppermute(value, axes, pairs)]
    all_to_all x1 -> x0, starting transfers between devices: 11.9 us -> none  [shards(): received = lax.all_to_all(partial, OWNERS, 0, 0)]
    ppermute x0 -> x6, waiting for transfers between devices: none -> 8.96 us  [passed(): return lax.ppermute(value, axes, pairs)]
    pallas_call x5 -> x10, Pallas kernels: 4.6 us -> 8.09 us  [call(): pl.pallas_call(kernel, out_shape=out_shape, in_specs=[VMEM] * len(operand...]
    pallas_call x1 -> x0, Pallas kernels: 3.44 us -> none  [correlate(): pl.pallas_call(correlate_kernel, grid=(2,), out_shape=jax.ShapeDtypeStruc...]
  transfers between devices with their start and end apart: 10 -> 15, of which waited for: 2 -> 6; matrix products, arithmetic and copies ran while one was open for 2% -> 2% of each run, Pallas kernels for 5% -> 10%
where the time goes in v2:
time: 52.9 us; the launch traced here: 52.3 us
  starting transfers between devices  31.4 us (59%)
  waiting for transfers between devices  9.13 us (17%)
  Pallas kernels  8.12 us (15%)
  local copies, waits for them, and re-layouts  2.74 us (5%)
  other arithmetic  0.72 us (1%)
    ppermute x6, starting transfers between devices, passed(): return lax.ppermute(value, axes, pairs)  15.4 us
    ppermute x8, starting transfers between devices, turned(): lax.ppermute(value, axis, [(i, (i + distance) % size) for i in range(size)])  15.3 us
    ppermute x6, waiting for transfers between devices, passed(): return lax.ppermute(value, axes, pairs)  8.96 us
    pallas_call x10, Pallas kernels, call(): pl.pallas_call(kernel, out_shape=out_shape, in_specs=[VMEM] * len(operand...  8.09 us
    unnamed x8, local copies, waits for them, and re-layouts  2.59 us
  transfers between devices with their start and end apart: 15, of which 6 were waited for; matrix products, arithmetic and copies ran while one was open for 2% of the time, Pallas kernels for 10%

profile of v2, /device:TPU:0, one launch (start us, length us, event | category | flops | bytes accessed | tf_op | source)
XLA Modules:
  0.0 52.3 jit_solution(6141451658536817427)
XLA Ops:
  0.0 0.9 %copy-done = f32[64,1024]{1,0:T(8,128)S(1)} copy-done((f32[64,1024]{1,0:T(8,128)S(1)}, f32[64,1024]{1,0:T(8,128)}, u32[]{:S(2)}) %copy-start) | copy-done | bytes 262168
  1.7 0.9 %copy-done.1 = f32[64,1024]{1,0:T(8,128)S(1)} copy-done((f32[64,1024]{1,0:T(8,128)S(1)}, f32[64,1024]{1,0:T(8,128)}, u32[]{:S(2)}) %copy-start.1) | copy-done | bytes 262168
  3.6 0.8 %shard_map.47 = (bf16[64,1152]{1,0:T(8,128)(2,1)S(1)}, bf16[64,1024]{1,0:T(8,128)(2,1)S(1)}) custom-call(f32[64,1024]{1,0:T(8,128)S(1)} %collective-permute-done.beside_ref, f32[64,640]{1,0:T(8,128)S(1)} %collective-permute-done.1.across_ref, bf16[256,1280]{1,0:T(8,128)(2,1)S(1)} %get-tuple-element.15.mat_high_ref, ...), custom_call_target="tpu_custom_call" | custom-call | flops 1000000000 | bytes 1048576 | tf_op jit(solution)/shard_map/pallas_call | solution.py:21
  4.4 4.2 %collective-permute-start.2 = (bf16[64,1024]{1,0:T(8,128)(2,1)S(1)}, bf16[64,1024]{1,0:T(8,128)(2,1)S(1)}, u32[]{:S(2)}, u32[]{:S(2)}) collective-permute-start(bf16[64,1024]{1,0:T(8,128)(2,1)S(1)} %get-tuple-element.19.refs_0_), channel_id=1, source_target_pairs={{0,48},{16,0},{32,16},{48,32},{1,49},{17,1},{33,17},{49,33},{2,50}... | collective-permute-start | bytes 393224 | tf_op jit(solution)/shard_map/ppermute | solution.py:279
  8.7 1.3 %collective-permute-start.4 = (bf16[64,1024]{1,0:T(8,128)(2,1)S(1)}, bf16[64,1024]{1,0:T(8,128)(2,1)S(1)}, u32[]{:S(2)}, u32[]{:S(2)}) collective-permute-start(bf16[64,1024]{1,0:T(8,128)(2,1)S(1)} %get-tuple-element.19.refs_0_), channel_id=1, source_target_pairs={{0,16},{16,32},{32,48},{48,0},{1,17},{17,33},{33,49},{49,1},{2,18}... | collective-permute-start | bytes 393224 | tf_op jit(solution)/shard_map/ppermute | solution.py:279
  9.9 3.2 %collective-permute-start.7 = (bf16[64,1152]{1,0:T(8,128)(2,1)S(1)}, bf16[64,1152]{1,0:T(8,128)(2,1)S(1)}, u32[]{:S(2)}, u32[]{:S(2)}) collective-permute-start(bf16[64,1152]{1,0:T(8,128)(2,1)S(1)} %get-tuple-element.20.mine_ref), channel_id=1, source_target_pairs={{0,64},{64,0},{1,65},{65,1},{2,66},{66,2},{3,67},{67,3},{4,68},{68... | collective-permute-start | bytes 442376 | tf_op jit(solution)/shard_map/ppermute | solution.py:279
  13.1 3.7 %collective-permute-start.5 = (bf16[64,1152]{1,0:T(8,128)(2,1)S(1)}, bf16[64,1152]{1,0:T(8,128)(2,1)S(1)}, u32[]{:S(2)}, u32[]{:S(2)}) collective-permute-start(bf16[64,1152]{1,0:T(8,128)(2,1)S(1)} %get-tuple-element.20.mine_ref), channel_id=1, source_target_pairs={{0,1},{1,0},{2,3},{3,2},{4,5},{5,4},{6,7},{7,6},{8,9},{9,8},{10,11... | collective-permute-start | bytes 442376 | tf_op jit(solution)/shard_map/ppermute | solution.py:279
  16.9 2.8 %collective-permute-start.6 = (bf16[192,1024]{1,0:T(8,128)(2,1)S(1)}, bf16[192,1024]{1,0:T(8,128)(2,1)S(1)}, u32[]{:S(2)}, u32[]{:S(2)}) collective-permute-start(bf16[192,1024]{1,0:T(8,128)(2,1)S(1)} %pad_maximum_fusion), channel_id=1, source_target_pairs={{0,1},{1,0},{2,3},{3,2},{4,5},{5,4},{6,7},{7,6},{8,9},{9,8},{10,11... | collective-permute-start | bytes 1179656 | tf_op jit(solution)/shard_map/ppermute | solution.py:279
  19.8 1.3 %shard_map.48.refs_6_ = bf16[1024,2048]{1,0:T(8,128)(2,1)S(1)} custom-call(bf16[64,1152]{1,0:T(8,128)(2,1)S(1)} %get-tuple-element.20.mine_ref, bf16[64,1152]{1,0:T(8,128)(2,1)S(1)} %collective-permute-done.5.theirs_ref.refs_4_), custom_call_target="tpu_custom_call" | custom-call | flops 2000000000 | bytes 1048576 | tf_op jit(solution)/shard_map/pallas_call | solution.py:21
  21.3 1.3 %shard_map.49.refs_7_ = bf16[1024,2048]{1,0:T(8,128)(2,1)S(1)} custom-call(bf16[64,1152]{1,0:T(8,128)(2,1)S(1)} %collective-permute-done.7.mine_ref, bf16[64,1152]{1,0:T(8,128)(2,1)S(1)} %collective-permute-done.8.theirs_ref), custom_call_target="tpu_custom_call" | custom-call | flops 2000000000 | bytes 1048576 | tf_op jit(solution)/shard_map/pallas_call | solution.py:21
  22.6 0.8 %shard_map.53 = bf16[512,256]{1,0:T(8,128)(2,1)S(1)} custom-call(bf16[64,1024]{1,0:T(8,128)(2,1)S(1)} %get-tuple-element.19.refs_0_, bf16[64,1024]{1,0:T(8,128)(2,1)S(1)} %collective-permute-done.2.refs_1_, bf16[64,1024]{1,0:T(8,128)(2,1)S(1)} %collective-permute-done.3.refs_2_, bf16[64,1024]{1,0:T(8,128)(2,1)S(1)} %collective-permute-done.4.refs_3_, ...), custom_call_target="tpu_custom_call" | custom-call | flops 1000000000 | bytes 1048576 | tf_op jit(solution)/shard_map/pallas_call | solution.py:21
  23.3 7.7 %collective-permute-start.11 = (bf16[512,256]{1,0:T(8,128)(2,1)S(1)}, bf16[512,256]{1,0:T(8,128)(2,1)S(1)}, u32[]{:S(2)}, u32[]{:S(2)}) collective-permute-start(bf16[512,256]{1,0:T(8,128)(2,1)S(1)} %shard_map.53), channel_id=1, source_target_pairs={{0,12},{1,67},{2,14},{3,1},{64,76},{65,3},{66,78},{67,65},{4,0},{5... | collective-permute-start | bytes 786440 | tf_op jit(solution)/shard_map/ppermute | solution.py:274
  31.8 0.9 %collective-permute-start.10 = (bf16[512,256]{1,0:T(8,128)(2,1)S(1)}, bf16[512,256]{1,0:T(8,128)(2,1)S(1)}, u32[]{:S(2)}, u32[]{:S(2)}) collective-permute-start(bf16[512,256]{1,0:T(8,128)(2,1)S(1)} %shard_map.52), channel_id=1, source_target_pairs={{0,8},{1,65},{2,10},{3,67},{64,72},{65,1},{66,74},{67,3},{4,12},{5... | collective-permute-start | bytes 786440 | tf_op jit(solution)/shard_map/ppermute | solution.py:274
  32.7 0.9 %shard_map.51 = bf16[512,256]{1,0:T(8,128)(2,1)S(1)} custom-call(bf16[64,1024]{1,0:T(8,128)(2,1)S(1)} %get-tuple-element.19.refs_0_, bf16[64,1024]{1,0:T(8,128)(2,1)S(1)} %collective-permute-done.2.refs_1_, bf16[64,1024]{1,0:T(8,128)(2,1)S(1)} %collective-permute-done.3.refs_2_, bf16[64,1024]{1,0:T(8,128)(2,1)S(1)} %collective-permute-done.4.refs_3_, ...), custom_call_target="tpu_custom_call" | custom-call | flops 1000000000 | bytes 1048576 | tf_op jit(solution)/shard_map/pallas_call | solution.py:21
  33.6 1.0 %collective-permute-start.9 = (bf16[512,256]{1,0:T(8,128)(2,1)S(1)}, bf16[512,256]{1,0:T(8,128)(2,1)S(1)}, u32[]{:S(2)}, u32[]{:S(2)}) collective-permute-start(bf16[512,256]{1,0:T(8,128)(2,1)S(1)} %shard_map.51), channel_id=1, source_target_pairs={{0,4},{1,3},{2,6},{3,65},{64,68},{65,67},{66,70},{67,1},{4,8},{5,7... | collective-permute-start | bytes 786440 | tf_op jit(solution)/shard_map/ppermute | solution.py:274
  34.6 0.8 %shard_map.50.own_ref = f32[512,256]{1,0:T(8,128)S(1)} custom-call(bf16[64,1024]{1,0:T(8,128)(2,1)S(1)} %get-tuple-element.19.refs_0_, bf16[64,1024]{1,0:T(8,128)(2,1)S(1)} %collective-permute-done.2.refs_1_, bf16[64,1024]{1,0:T(8,128)(2,1)S(1)} %collective-permute-done.3.refs_2_, bf16[64,1024]{1,0:T(8,128)(2,1)S(1)} %collective-permute-done.4.refs_3_, ...), custom_call_target="tpu_custom_call" | custom-call | flops 1000000000 | bytes 1048576 | tf_op jit(solution)/shard_map/pallas_call | solution.py:21
  35.4 2.4 %collective-permute-done.11.third_ref = bf16[512,256]{1,0:T(8,128)(2,1)S(1)} collective-permute-done((bf16[512,256]{1,0:T(8,128)(2,1)S(1)}, bf16[512,256]{1,0:T(8,128)(2,1)S(1)}, u32[]{:S(2)}, u32[]{:S(2)}) %collective-permute-start.11) | collective-permute-done | bytes 262176 | tf_op jit(solution)/shard_map/ppermute | solution.py:274
  37.8 2.1 %collective-permute-done.10.second_ref = bf16[512,256]{1,0:T(8,128)(2,1)S(1)} collective-permute-done((bf16[512,256]{1,0:T(8,128)(2,1)S(1)}, bf16[512,256]{1,0:T(8,128)(2,1)S(1)}, u32[]{:S(2)}, u32[]{:S(2)}) %collective-permute-start.10) | collective-permute-done | bytes 262176 | tf_op jit(solution)/shard_map/ppermute | solution.py:274
  39.9 2.7 %collective-permute-done.9.first_ref = bf16[512,256]{1,0:T(8,128)(2,1)S(1)} collective-permute-done((bf16[512,256]{1,0:T(8,128)(2,1)S(1)}, bf16[512,256]{1,0:T(8,128)(2,1)S(1)}, u32[]{:S(2)}, u32[]{:S(2)}) %collective-permute-start.9) | collective-permute-done | bytes 262176 | tf_op jit(solution)/shard_map/ppermute | solution.py:274
  43.0 3.3 %collective-permute-start.13 = (bf16[2,128,256]{2,1,0:T(8,128)(2,1)S(1)}, bf16[2,128,256]{2,1,0:T(8,128)(2,1)S(1)}, u32[]{:S(2)}, u32[]{:S(2)}) collective-permute-start(bf16[2,128,256]{2,1,0:T(8,128)(2,1)S(1)} %get-tuple-element.23), channel_id=1, source_target_pairs={{0,64},{1,9},{2,66},{3,11},{64,0},{65,73},{66,2},{67,75},{4,68},{5... | collective-permute-start | bytes 393224 | tf_op jit(solution)/shard_map/ppermute | solution.py:274
  46.2 2.5 %collective-permute-start.14 = (bf16[2,128,256]{2,1,0:T(8,128)(2,1)S(1)}, bf16[2,128,256]{2,1,0:T(8,128)(2,1)S(1)}, u32[]{:S(2)}, u32[]{:S(2)}) collective-permute-start(bf16[2,128,256]{2,1,0:T(8,128)(2,1)S(1)} %get-tuple-element.24), channel_id=1, source_target_pairs={{0,66},{1,13},{2,0},{3,15},{64,2},{65,77},{66,64},{67,79},{4,70},{... | collective-permute-start | bytes 393224 | tf_op jit(solution)/shard_map/ppermute | solution.py:274
  49.6 0.9 %collective-permute-done.13.second_ref = bf16[2,128,256]{2,1,0:T(8,128)(2,1)S(1)} collective-permute-done((bf16[2,128,256]{2,1,0:T(8,128)(2,1)S(1)}, bf16[2,128,256]{2,1,0:T(8,128)(2,1)S(1)}, u32[]{:S(2)}, u32[]{:S(2)}) %collective-permute-start.13) | collective-permute-done | bytes 131104 | tf_op jit(solution)/shard_map/ppermute | solution.py:274
  50.5 0.9 %collective-permute-done.14.third_ref = bf16[2,128,256]{2,1,0:T(8,128)(2,1)S(1)} collective-permute-done((bf16[2,128,256]{2,1,0:T(8,128)(2,1)S(1)}, bf16[2,128,256]{2,1,0:T(8,128)(2,1)S(1)}, u32[]{:S(2)}, u32[]{:S(2)}) %collective-permute-start.14) | collective-permute-done | bytes 131104 | tf_op jit(solution)/shard_map/ppermute | solution.py:274
  51.4 0.9 %shard_map.55 = f32[128,512]{1,0:T(8,128)} custom-call(f32[2,128,256]{2,1,0:T(8,128)S(1)} %get-tuple-element.21.own_ref, bf16[2,128,256]{2,1,0:T(8,128)(2,1)S(1)} %collective-permute-done.12.first_ref, bf16[2,128,256]{2,1,0:T(8,128)(2,1)S(1)} %collective-permute-done.13.second_ref, bf16[2,128,256]{2,1,0:T(8,128)(2,1)S(1)} %collective-permute-done.14.third_ref, ...), custom_call_target="tpu_custom_call" | custom-call | flops 100000000 | bytes 1048576 | tf_op jit(solution)/shard_map/pallas_call | solution.py:21
  (29 shorter events, 3.9 us)
Async XLA Ops:
  0.0 3.6 %collective-permute-start = (f32[64,1024]{1,0:T(8,128)}, f32[64,1024]{1,0:T(8,128)S(1)}, u32[]{:S(2)}, u32[]{:S(2)}) collective-permute-start(f32[64,1024]{1,0:T(8,128)} %own_ref.3), channel_id=1, source_target_pairs={{0,1},{1,0},{2,3},{3,2},{4,5},{5,4},{6,7},{7,6},{8,9},{9,8},{10,11... | collective-permute-start | bytes 786440 | tf_op jit(solution)/shard_map/ppermute | solution.py:279
  0.0 1.0 %copy-start = (f32[64,1024]{1,0:T(8,128)S(1)}, f32[64,1024]{1,0:T(8,128)}, u32[]{:S(2)}) copy-start(f32[64,1024]{1,0:T(8,128)} %own_ref.3) | copy-start | bytes 786436
  1.0 2.6 %collective-permute-start.1 = (f32[64,640]{1,0:T(8,128)S(1)}, f32[64,640]{1,0:T(8,128)S(1)}, u32[]{:S(2)}, u32[]{:S(2)}) collective-permute-start(f32[64,640]{1,0:T(8,128)S(1)} %edge.1), channel_id=1, source_target_pairs={{1,2},{3,4},{5,6},{7,8},{9,10},{11,12},{13,14},{2,1},{4,3},{6,5},{... | collective-permute-start | bytes 491528 | tf_op jit(solution)/shard_map/ppermute | solution.py:291
  1.7 1.0 %copy-start.1 = (f32[64,1024]{1,0:T(8,128)S(1)}, f32[64,1024]{1,0:T(8,128)}, u32[]{:S(2)}) copy-start(f32[64,1024]{1,0:T(8,128)} %own_ref.3) | copy-start | bytes 786436
  2.6 0.7 %copy-start.3 = (f32[1024]{0:T(1024)S(1)}, f32[1024]{0:T(1024)}, u32[]{:S(2)}) copy-start(f32[1024]{0:T(1024)} %param.5) | copy-start | bytes 12292
  4.4 12.4 %collective-permute-start.2 = (bf16[64,1024]{1,0:T(8,128)(2,1)S(1)}, bf16[64,1024]{1,0:T(8,128)(2,1)S(1)}, u32[]{:S(2)}, u32[]{:S(2)}) collective-permute-start(bf16[64,1024]{1,0:T(8,128)(2,1)S(1)} %get-tuple-element.19.refs_0_), channel_id=1, source_target_pairs={{0,48},{16,0},{32,16},{48,32},{1,49},{17,1},{33,17},{49,33},{2,50}... | collective-permute-start | bytes 393224 | tf_op jit(solution)/shard_map/ppermute | solution.py:279
  8.7 8.2 %collective-permute-start.3 = (bf16[64,1024]{1,0:T(8,128)(2,1)S(1)}, bf16[64,1024]{1,0:T(8,128)(2,1)S(1)}, u32[]{:S(2)}, u32[]{:S(2)}) collective-permute-start(bf16[64,1024]{1,0:T(8,128)(2,1)S(1)} %get-tuple-element.19.refs_0_), channel_id=1, source_target_pairs={{0,32},{16,48},{32,0},{48,16},{1,33},{17,49},{33,1},{49,17},{2,34}... | collective-permute-start | bytes 393224 | tf_op jit(solution)/shard_map/ppermute | solution.py:279
  8.7 8.2 %collective-permute-start.4 = (bf16[64,1024]{1,0:T(8,128)(2,1)S(1)}, bf16[64,1024]{1,0:T(8,128)(2,1)S(1)}, u32[]{:S(2)}, u32[]{:S(2)}) collective-permute-start(bf16[64,1024]{1,0:T(8,128)(2,1)S(1)} %get-tuple-element.19.refs_0_), channel_id=1, source_target_pairs={{0,16},{16,32},{32,48},{48,0},{1,17},{17,33},{33,49},{49,1},{2,18}... | collective-permute-start | bytes 393224 | tf_op jit(solution)/shard_map/ppermute | solution.py:279
  9.9 9.8 %collective-permute-start.7 = (bf16[64,1152]{1,0:T(8,128)(2,1)S(1)}, bf16[64,1152]{1,0:T(8,128)(2,1)S(1)}, u32[]{:S(2)}, u32[]{:S(2)}) collective-permute-start(bf16[64,1152]{1,0:T(8,128)(2,1)S(1)} %get-tuple-element.20.mine_ref), channel_id=1, source_target_pairs={{0,64},{64,0},{1,65},{65,1},{2,66},{66,2},{3,67},{67,3},{4,68},{68... | collective-permute-start | bytes 442376 | tf_op jit(solution)/shard_map/ppermute | solution.py:279
  13.1 6.7 %collective-permute-start.5 = (bf16[64,1152]{1,0:T(8,128)(2,1)S(1)}, bf16[64,1152]{1,0:T(8,128)(2,1)S(1)}, u32[]{:S(2)}, u32[]{:S(2)}) collective-permute-start(bf16[64,1152]{1,0:T(8,128)(2,1)S(1)} %get-tuple-element.20.mine_ref), channel_id=1, source_target_pairs={{0,1},{1,0},{2,3},{3,2},{4,5},{5,4},{6,7},{7,6},{8,9},{9,8},{10,11... | collective-permute-start | bytes 442376 | tf_op jit(solution)/shard_map/ppermute | solution.py:279
  16.9 5.7 %collective-permute-start.6 = (bf16[192,1024]{1,0:T(8,128)(2,1)S(1)}, bf16[192,1024]{1,0:T(8,128)(2,1)S(1)}, u32[]{:S(2)}, u32[]{:S(2)}) collective-permute-start(bf16[192,1024]{1,0:T(8,128)(2,1)S(1)} %pad_maximum_fusion), channel_id=1, source_target_pairs={{0,1},{1,0},{2,3},{3,2},{4,5},{5,4},{6,7},{7,6},{8,9},{9,8},{10,11... | collective-permute-start | bytes 1179656 | tf_op jit(solution)/shard_map/ppermute | solution.py:279
  19.7 1.6 %collective-permute-start.8 = (bf16[64,1152]{1,0:T(8,128)(2,1)S(1)}, bf16[64,1152]{1,0:T(8,128)(2,1)S(1)}, u32[]{:S(2)}, u32[]{:S(2)}) collective-permute-start(bf16[64,1152]{1,0:T(8,128)(2,1)S(1)} %collective-permute-done.7.mine_ref), channel_id=1, source_target_pairs={{0,1},{1,0},{2,3},{3,2},{4,5},{5,4},{6,7},{7,6},{8,9},{9,8},{10,11... | collective-permute-start | bytes 442376 | tf_op jit(solution)/shard_map/ppermute | solution.py:279
  23.3 14.4 %collective-permute-start.11 = (bf16[512,256]{1,0:T(8,128)(2,1)S(1)}, bf16[512,256]{1,0:T(8,128)(2,1)S(1)}, u32[]{:S(2)}, u32[]{:S(2)}) collective-permute-start(bf16[512,256]{1,0:T(8,128)(2,1)S(1)} %shard_map.53), channel_id=1, source_target_pairs={{0,12},{1,67},{2,14},{3,1},{64,76},{65,3},{66,78},{67,65},{4,0},{5... | collective-permute-start | bytes 786440 | tf_op jit(solution)/shard_map/ppermute | solution.py:274
  31.8 8.1 %collective-permute-start.10 = (bf16[512,256]{1,0:T(8,128)(2,1)S(1)}, bf16[512,256]{1,0:T(8,128)(2,1)S(1)}, u32[]{:S(2)}, u32[]{:S(2)}) collective-permute-start(bf16[512,256]{1,0:T(8,128)(2,1)S(1)} %shard_map.52), channel_id=1, source_target_pairs={{0,8},{1,65},{2,10},{3,67},{64,72},{65,1},{66,74},{67,3},{4,12},{5... | collective-permute-start | bytes 786440 | tf_op jit(solution)/shard_map/ppermute | solution.py:274
  33.6 17.8 %copy-start.2 = (f32[2,64,512]{2,1,0:T(8,128)S(1)}, f32[2,64,512]{2,1,0:T(8,128)}, u32[]{:S(2)}) copy-start(f32[2,64,512]{2,1,0:T(8,128)} %param.7) | copy-start | bytes 786436
  33.6 8.9 %collective-permute-start.9 = (bf16[512,256]{1,0:T(8,128)(2,1)S(1)}, bf16[512,256]{1,0:T(8,128)(2,1)S(1)}, u32[]{:S(2)}, u32[]{:S(2)}) collective-permute-start(bf16[512,256]{1,0:T(8,128)(2,1)S(1)} %shard_map.51), channel_id=1, source_target_pairs={{0,4},{1,3},{2,6},{3,65},{64,68},{65,67},{66,70},{67,1},{4,8},{5,7... | collective-permute-start | bytes 786440 | tf_op jit(solution)/shard_map/ppermute | solution.py:274
  42.9 6.7 %collective-permute-start.12 = (bf16[2,128,256]{2,1,0:T(8,128)(2,1)S(1)}, bf16[2,128,256]{2,1,0:T(8,128)(2,1)S(1)}, u32[]{:S(2)}, u32[]{:S(2)}) collective-permute-start(bf16[2,128,256]{2,1,0:T(8,128)(2,1)S(1)} %get-tuple-element.22), channel_id=1, source_target_pairs={{0,2},{1,5},{2,64},{3,7},{64,66},{65,69},{66,0},{67,71},{4,6},{5,9... | collective-permute-start | bytes 393224 | tf_op jit(solution)/shard_map/ppermute | solution.py:274
  43.0 7.6 %collective-permute-start.13 = (bf16[2,128,256]{2,1,0:T(8,128)(2,1)S(1)}, bf16[2,128,256]{2,1,0:T(8,128)(2,1)S(1)}, u32[]{:S(2)}, u32[]{:S(2)}) collective-permute-start(bf16[2,128,256]{2,1,0:T(8,128)(2,1)S(1)} %get-tuple-element.23), channel_id=1, source_target_pairs={{0,64},{1,9},{2,66},{3,11},{64,0},{65,73},{66,2},{67,75},{4,68},{5... | collective-permute-start | bytes 393224 | tf_op jit(solution)/shard_map/ppermute | solution.py:274
  46.2 5.2 %collective-permute-start.14 = (bf16[2,128,256]{2,1,0:T(8,128)(2,1)S(1)}, bf16[2,128,256]{2,1,0:T(8,128)(2,1)S(1)}, u32[]{:S(2)}, u32[]{:S(2)}) collective-permute-start(bf16[2,128,256]{2,1,0:T(8,128)(2,1)S(1)} %get-tuple-element.24), channel_id=1, source_target_pairs={{0,66},{1,13},{2,0},{3,15},{64,2},{65,77},{66,64},{67,79},{4,70},{... | collective-permute-start | bytes 393224 | tf_op jit(solution)/shard_map/ppermute | solution.py:274

commit v3 on v2

--- a/solution.py
+++ b/solution.py
@@ -15,6 +15,7 @@
 TILE = 256
 PAD = 128
 MIB = 1 << 20
+SCALE = 4096.0
 
 
 def call(kernel, out_shape, operands, mib, flops):
@@ -26,24 +27,6 @@
         compiler_params=pltpu.CompilerParams(vmem_limit_bytes=mib * MIB),
         cost_estimate=pl.CostEstimate(flops=flops, bytes_accessed=MIB, transcendentals=0),
     )(*operands)
-
-
-def edge_kernel(own_ref, edge_ref):
-    width = edge_ref.shape[1]
-    lower = lax.axis_index("c") == 0
-    pl.when(lower)(lambda: pltpu.sync_copy(own_ref.at[:, :width], edge_ref))
-    pl.when(jnp.logical_not(lower))(lambda: pltpu.sync_copy(own_ref.at[:, own_ref.shape[1] - width :], edge_ref))
-
-
-def facing_edge(own, width):
-    return pl.pallas_call(
-        edge_kernel,
-        out_shape=jax.ShapeDtypeStruct((own.shape[0], width), own.dtype),
-        in_specs=[pl.BlockSpec(memory_space=pl.ANY)],
-        out_specs=VMEM,
-        compiler_params=pltpu.CompilerParams(vmem_limit_bytes=2 * MIB),
-        name="edge",
-    )(own)
 
 
 def split(value):
@@ -114,35 +97,25 @@
     )
 
 
-def rows_kernel(lag_count, mine_ref, theirs_ref, rows_ref):
-    channels, seg_len = mine_ref.shape[0], mine_ref.shape[1] - PAD
+def rows_kernel(lag_count, segment_ref, rows_ref):
+    channels = segment_ref.shape[0]
     core = lax.axis_index("c")
-    mine, theirs = mine_ref[...], theirs_ref[...]
-    first = jnp.where(core == 0, mine, theirs)
-    second = jnp.where(core == 0, theirs, mine)
-    both = jnp.concatenate([first, second[:, PAD:]], axis=1)
-    both = jnp.where(core == 0, both, pltpu.roll(both, 2, 1))
+    segment = segment_ref[...]
+    segment = jnp.where(core == 0, segment, pltpu.roll(segment, 2, 1))
+    groups = lag_count // 2
     for index in range(lag_count):
         group, second = index // 2, index % 2
         lag = 4 * group + second
-        moved = both if lag == 0 else pltpu.roll(both, lag, 1)
-        groups = lag_count // 2
+        moved = segment if lag == 0 else pltpu.roll(segment, lag, 1)
         place = jnp.where(core == 0, group, group % 2 * (groups // 2) + group // 2)
         at = pl.ds(pl.multiple_of((2 * place + second) * channels, channels), channels)
-        for k in range(2):
-            begin = pl.multiple_of((core if k == 0 else 1 - core) * seg_len, seg_len)
-            rows_ref[at, pl.ds(begin, seg_len)] = moved[:, PAD + k * seg_len : PAD + (k + 1) * seg_len]
-
-
-def lagged_rows(mine, theirs, lag_count):
-    channels, width = mine.shape
-    return call(
-        functools.partial(rows_kernel, lag_count),
-        jax.ShapeDtypeStruct((lag_count * channels, 2 * (width - PAD)), jnp.bfloat16),
-        (mine, theirs),
-        8,
-        2 * 10**9,
-    )
+        rows_ref[at, :] = moved[:, PAD:]
+
+
+def lagged_rows(segment, lag_count):
+    channels, width = segment.shape
+    shape = jax.ShapeDtypeStruct((lag_count * channels, width - PAD), jnp.bfloat16)
+    return call(functools.partial(rows_kernel, lag_count), shape, (segment,), 4, 10**9)
 
 
 def position():
@@ -150,23 +123,26 @@
     return core, x, y
 
 
-def chunk_kernel(distance, *refs):
-    *piece_refs, mine_ref, other_ref, out_ref = refs
-    seg_len = piece_refs[0].shape[1]
+def chunk_kernel(distance, halves, *refs):
+    *refs, out_ref = refs
+    start_refs = [] if 0 in halves else [refs.pop()]
+    row_refs = refs[-2 * len(halves) :]
+    mine_ref, other_ref = row_refs[: len(halves)], row_refs[len(halves) :]
+    col_refs = refs[: -2 * len(halves)]
+    seg_len = col_refs[0].shape[1] if 0 in halves else col_refs[-1].shape[1]
     rows = out_ref.shape[0] // 2
     core, x, y = position()
     yh = lax.axis_index("yh")
     to_x, to_y = lax.rem(x + distance, 4), lax.rem(y + distance, 4)
 
     def fill(first_ref, second_ref, first_at, second_at):
-        total = 0.0
-        for k in range(2):
-            refs = piece_refs[-2:] if k else piece_refs[:-2]
-            cols = jnp.concatenate([ref[:, ref.shape[1] - seg_len :] for ref in refs], axis=0)
-            part = slice(k * seg_len, (k + 1) * seg_len)
+        total = sum(ref[...] for ref in start_refs)
+        for k, half in enumerate(halves):
+            parts = col_refs[-2:] if half else col_refs[:4]
+            cols = jnp.concatenate([ref[:, ref.shape[1] - seg_len :] for ref in parts], axis=0)
             left = jnp.concatenate(
                 [
-                    ref[pl.ds(pl.multiple_of(at, rows), rows), part]
+                    ref[k][pl.ds(pl.multiple_of(at, rows), rows), :]
                     for ref, at in ((first_ref, first_at), (second_ref, second_at))
                 ],
                 axis=0,
@@ -196,13 +172,15 @@
         fill(other_ref, other_ref, along_y, along_y + rows)
 
 
-def chunk(pieces, mine_rows, other_rows, distance):
+def chunk(pieces, rows, distance, halves=(0, 1), start=()):
     width = pieces[0].shape[0] * (len(pieces) - 2)
-    kind = jnp.bfloat16 if distance else jnp.float32
+    whole = distance == 0 or 1 not in halves
+    cols = (pieces[:-2] if 0 in halves else []) + (pieces[-2:] if 1 in halves else [])
+    rows = [rows[2 * k + half] for k in range(2) for half in halves]
     return call(
-        functools.partial(chunk_kernel, distance),
-        jax.ShapeDtypeStruct((mine_rows.shape[0] // 2, width), kind),
-        (*pieces, mine_rows, other_rows),
+        functools.partial(chunk_kernel, distance, halves),
+        jax.ShapeDtypeStruct((rows[0].shape[0] // 2, width), jnp.float32 if whole else jnp.bfloat16),
+        (*cols, *rows, *start),
         6,
         10**9,
     )
@@ -284,11 +262,13 @@
     half_taps = whitening.shape[0] // 2
     segments = lax.axis_size(TIME)
     lags = old_stack.shape[0]
-    z, yh, zs = lax.axis_index("z"), lax.axis_index("yh"), lax.axis_size("z")
+    core, z, yh, zs = lax.axis_index("c"), lax.axis_index("z"), lax.axis_index("yh"), lax.axis_size("z")
     reach = half_taps + PAD
-    edge = facing_edge(raw_strain, reach)
+    edge = jnp.where(core == 0, raw_strain[:, :reach], raw_strain[:, seg_len - reach :])
+    edge = (edge * SCALE).astype(jnp.float16)
     pairs = [(i, i + 1) for i in range(1, segments - 1, 2)]
     across = lax.ppermute(edge, TIME, pairs + [(b, a) for a, b in pairs])
+    across = across.astype(jnp.float32) * (1.0 / SCALE)
     beside = turned(raw_strain, "c", 1)
     prepared = prepare(whitening, raw_strain)
     mine, own = filter_segment(beside, across, prepared, half_taps)
@@ -301,11 +281,12 @@
     pieces += [mine_swapped, turned(jnp.concatenate(pieces[1:], axis=0), "c", 1)]
     lag_count = lags * segments // 2
     other_swapped = turned(other, "c", 1)
-    mine_rows = lagged_rows(mine, mine_swapped, lag_count)
-    other_rows = lagged_rows(other, other_swapped, lag_count)
+    sources = (mine, mine_swapped, other, other_swapped)
+    rows = [lagged_rows(segment, lag_count) for segment in sources]
     sums = {}
-    for d in (2, 1, 3, 0):
-        sums[d] = chunk(pieces, mine_rows, other_rows, d)
+    lead = chunk(pieces, rows, 1, (0,))
+    for d in (1, 3, 2, 0):
+        sums[d] = chunk(pieces, rows, d, (1,), (lead,)) if d == 1 else chunk(pieces, rows, d)
         if d:
             sums[d] = passed(sums[d], d, 0)
     own_part, *parts = middle(*[sums[d] for d in range(4)])

time: 52.9 us -> 52.4 us (level)
  starting transfers between devices: 31.4 us -> 27.9 us
  waiting for transfers between devices: 9.13 us -> 11.5 us
  other arithmetic: 0.72 us -> 1.76 us
  local copies, waits for them, and re-layouts: 2.74 us -> 1.79 us
    ppermute x8, starting transfers between devices: 15.3 us -> 12.8 us  [turned(): lax.ppermute(value, axis, [(i, (i + distance) % size) for i in range(size)])]
    ppermute x8, waiting for transfers between devices: 0.17 us -> 2.12 us  [turned(): lax.ppermute(value, axis, [(i, (i + distance) % size) for i in range(size)])]
    ppermute x6, starting transfers between devices: 15.4 us -> 14.4 us  [passed(): return lax.ppermute(value, axes, pairs)]
    convert_element_type x0 -> x1, other arithmetic: none -> 1.02 us  [shards(): edge = (edge * SCALE).astype(jnp.float16)]
    unnamed x8 -> x6, local copies, waits for them, and re-layouts: 2.59 us -> 1.64 us
    pallas_call x10 -> x13, Pallas kernels: 8.09 us -> 8.56 us  [call(): pl.pallas_call(kernel, out_shape=out_shape, in_specs=[VMEM] * len(operand...]
  transfers between devices with their start and end apart: 15 -> 15, of which waited for: 6 -> 6; matrix products, arithmetic and copies ran while one was open for 2% -> 4% of each run, Pallas kernels for 10% -> 11%
where the time goes in v3:
time: 52.4 us; the launch traced here: 51.7 us
  starting transfers between devices  27.9 us (53%)
  waiting for transfers between devices  11.5 us (22%)
  Pallas kernels  8.56 us (16%)
  local copies, waits for them, and re-layouts  1.79 us (3%)
  other arithmetic  1.76 us (3%)
    ppermute x6, starting transfers between devices, passed(): return lax.ppermute(value, axes, pairs)  14.4 us
    ppermute x8, starting transfers between devices, turned(): lax.ppermute(value, axis, [(i, (i + distance) % size) for i in range(size)])  12.8 us
    ppermute x6, waiting for transfers between devices, passed(): return lax.ppermute(value, axes, pairs)  9.42 us
    pallas_call x13, Pallas kernels, call(): pl.pallas_call(kernel, out_shape=out_shape, in_specs=[VMEM] * len(operand...  8.56 us
    ppermute x8, waiting for transfers between devices, turned(): lax.ppermute(value, axis, [(i, (i + distance) % size) for i in range(size)])  2.12 us
    unnamed x6, local copies, waits for them, and re-layouts  1.64 us
  transfers between devices with their start and end apart: 15, of which 6 were waited for; matrix products, arithmetic and copies ran while one was open for 4% of the time, Pallas kernels for 11%

profile of v3, /device:TPU:0, one launch (start us, length us, event | category | flops | bytes accessed | tf_op | source)
XLA Modules:
  0.0 51.7 jit_solution(1508058882770157023)
XLA Ops:
  0.0 1.0 %multiply_convert_fusion = f16[64,640]{1,0:T(8,128)(2,1)S(1)} fusion(f32[64,1024]{1,0:T(8,128)} %own_ref.1, pred[]{:T(512)S(6)} %eq.3), kind=kLoop, calls=%fused_computation.2 | loop fusion | flops 122880 | bytes 409601 | tf_op jit(solution)/shard_map/convert_element_type | solution.py:268
  1.7 0.9 %copy-done = f32[64,1024]{1,0:T(8,128)S(1)} copy-done((f32[64,1024]{1,0:T(8,128)S(1)}, f32[64,1024]{1,0:T(8,128)}, u32[]{:S(2)}) %copy-start) | copy-done | bytes 262168
  3.7 0.8 %shard_map.47 = (bf16[64,1152]{1,0:T(8,128)(2,1)S(1)}, bf16[64,1024]{1,0:T(8,128)(2,1)S(1)}) custom-call(f32[64,1024]{1,0:T(8,128)S(1)} %collective-permute-done.beside_ref, f32[64,640]{1,0:T(8,128)S(1)} %convert_multiply_fusion.across_ref, bf16[256,1280]{1,0:T(8,128)(2,1)S(1)} %get-tuple-element.15.mat_high_ref, ...), custom_call_target="tpu_custom_call" | custom-call | flops 1000000000 | bytes 1048576 | tf_op jit(solution)/shard_map/pallas_call | solution.py:22
  4.5 4.2 %collective-permute-start.2 = (bf16[64,1024]{1,0:T(8,128)(2,1)S(1)}, bf16[64,1024]{1,0:T(8,128)(2,1)S(1)}, u32[]{:S(2)}, u32[]{:S(2)}) collective-permute-start(bf16[64,1024]{1,0:T(8,128)(2,1)S(1)} %get-tuple-element.19.refs_0_), channel_id=1, source_target_pairs={{0,48},{16,0},{32,16},{48,32},{1,49},{17,1},{33,17},{49,33},{2,50}... | collective-permute-start | bytes 393224 | tf_op jit(solution)/shard_map/ppermute | solution.py:257
  8.7 1.3 %collective-permute-start.4 = (bf16[64,1024]{1,0:T(8,128)(2,1)S(1)}, bf16[64,1024]{1,0:T(8,128)(2,1)S(1)}, u32[]{:S(2)}, u32[]{:S(2)}) collective-permute-start(bf16[64,1024]{1,0:T(8,128)(2,1)S(1)} %get-tuple-element.19.refs_0_), channel_id=1, source_target_pairs={{0,16},{16,32},{32,48},{48,0},{1,17},{17,33},{33,49},{49,1},{2,18}... | collective-permute-start | bytes 393224 | tf_op jit(solution)/shard_map/ppermute | solution.py:257
  10.0 2.8 %collective-permute-start.5 = (bf16[64,1152]{1,0:T(8,128)(2,1)S(1)}, bf16[64,1152]{1,0:T(8,128)(2,1)S(1)}, u32[]{:S(2)}, u32[]{:S(2)}) collective-permute-start(bf16[64,1152]{1,0:T(8,128)(2,1)S(1)} %get-tuple-element.20.segment_ref), channel_id=1, source_target_pairs={{0,1},{1,0},{2,3},{3,2},{4,5},{5,4},{6,7},{7,6},{8,9},{9,8},{10,11... | collective-permute-start | bytes 442376 | tf_op jit(solution)/shard_map/ppermute | solution.py:257
  12.8 3.2 %collective-permute-start.7 = (bf16[64,1152]{1,0:T(8,128)(2,1)S(1)}, bf16[64,1152]{1,0:T(8,128)(2,1)S(1)}, u32[]{:S(2)}, u32[]{:S(2)}) collective-permute-start(bf16[64,1152]{1,0:T(8,128)(2,1)S(1)} %get-tuple-element.20.segment_ref), channel_id=1, source_target_pairs={{0,64},{64,0},{1,65},{65,1},{2,66},{66,2},{3,67},{67,3},{4,68},{68... | collective-permute-start | bytes 442376 | tf_op jit(solution)/shard_map/ppermute | solution.py:257
  16.0 2.1 %collective-permute-done.4.refs_3_ = bf16[64,1024]{1,0:T(8,128)(2,1)S(1)} collective-permute-done((bf16[64,1024]{1,0:T(8,128)(2,1)S(1)}, bf16[64,1024]{1,0:T(8,128)(2,1)S(1)}, u32[]{:S(2)}, u32[]{:S(2)}) %collective-permute-start.4) | collective-permute-done | bytes 131104 | tf_op jit(solution)/shard_map/ppermute | solution.py:257
  18.1 1.2 %collective-permute-start.6 = (bf16[192,1024]{1,0:T(8,128)(2,1)S(1)}, bf16[192,1024]{1,0:T(8,128)(2,1)S(1)}, u32[]{:S(2)}, u32[]{:S(2)}) collective-permute-start(bf16[192,1024]{1,0:T(8,128)(2,1)S(1)} %pad_maximum_fusion), channel_id=1, source_target_pairs={{0,1},{1,0},{2,3},{3,2},{4,5},{5,4},{6,7},{7,6},{8,9},{9,8},{10,11... | collective-permute-start | bytes 1179656 | tf_op jit(solution)/shard_map/ppermute | solution.py:257
  22.3 0.7 %shard_map.51.refs_9_.refs_3_ = bf16[1024,1024]{1,0:T(8,128)(2,1)S(1)} custom-call(bf16[64,1152]{1,0:T(8,128)(2,1)S(1)} %collective-permute-done.8.segment_ref), custom_call_target="tpu_custom_call" | custom-call | flops 1000000000 | bytes 1048576 | tf_op jit(solution)/shard_map/pallas_call | solution.py:22
  23.0 0.8 %shard_map.56 = bf16[512,256]{1,0:T(8,128)(2,1)S(1)} custom-call(bf16[64,1024]{1,0:T(8,128)(2,1)S(1)} %get-tuple-element.19.refs_0_, bf16[64,1024]{1,0:T(8,128)(2,1)S(1)} %collective-permute-done.2.refs_1_, bf16[64,1024]{1,0:T(8,128)(2,1)S(1)} %collective-permute-done.3.refs_2_, bf16[64,1024]{1,0:T(8,128)(2,1)S(1)} %collective-permute-done.4.refs_3_, ...), custom_call_target="tpu_custom_call" | custom-call | flops 1000000000 | bytes 1048576 | tf_op jit(solution)/shard_map/pallas_call | solution.py:22
  23.8 6.5 %collective-permute-start.11 = (bf16[512,256]{1,0:T(8,128)(2,1)S(1)}, bf16[512,256]{1,0:T(8,128)(2,1)S(1)}, u32[]{:S(2)}, u32[]{:S(2)}) collective-permute-start(bf16[512,256]{1,0:T(8,128)(2,1)S(1)} %shard_map.56), channel_id=1, source_target_pairs={{0,12},{1,67},{2,14},{3,1},{64,76},{65,3},{66,78},{67,65},{4,0},{5... | collective-permute-start | bytes 786440 | tf_op jit(solution)/shard_map/ppermute | solution.py:252
  30.3 0.8 %shard_map.55 = bf16[512,256]{1,0:T(8,128)(2,1)S(1)} custom-call(bf16[64,1024]{1,0:T(8,128)(2,1)S(1)} %get-tuple-element.19.refs_0_, bf16[64,1024]{1,0:T(8,128)(2,1)S(1)} %collective-permute-done.2.refs_1_, bf16[64,1024]{1,0:T(8,128)(2,1)S(1)} %collective-permute-done.3.refs_2_, bf16[64,1024]{1,0:T(8,128)(2,1)S(1)} %collective-permute-done.4.refs_3_, ...), custom_call_target="tpu_custom_call" | custom-call | flops 1000000000 | bytes 1048576 | tf_op jit(solution)/shard_map/pallas_call | solution.py:22
  31.1 1.1 %collective-permute-start.10 = (bf16[512,256]{1,0:T(8,128)(2,1)S(1)}, bf16[512,256]{1,0:T(8,128)(2,1)S(1)}, u32[]{:S(2)}, u32[]{:S(2)}) collective-permute-start(bf16[512,256]{1,0:T(8,128)(2,1)S(1)} %shard_map.55), channel_id=1, source_target_pairs={{0,8},{1,65},{2,10},{3,67},{64,72},{65,1},{66,74},{67,3},{4,12},{5... | collective-permute-start | bytes 786440 | tf_op jit(solution)/shard_map/ppermute | solution.py:252
  32.6 1.0 %collective-permute-start.9 = (bf16[512,256]{1,0:T(8,128)(2,1)S(1)}, bf16[512,256]{1,0:T(8,128)(2,1)S(1)}, u32[]{:S(2)}, u32[]{:S(2)}) collective-permute-start(bf16[512,256]{1,0:T(8,128)(2,1)S(1)} %shard_map.54), channel_id=1, source_target_pairs={{0,4},{1,3},{2,6},{3,65},{64,68},{65,67},{66,70},{67,1},{4,8},{5,7... | collective-permute-start | bytes 786440 | tf_op jit(solution)/shard_map/ppermute | solution.py:252
  33.6 0.8 %shard_map.52.own_ref = f32[512,256]{1,0:T(8,128)S(1)} custom-call(bf16[64,1024]{1,0:T(8,128)(2,1)S(1)} %get-tuple-element.19.refs_0_, bf16[64,1024]{1,0:T(8,128)(2,1)S(1)} %collective-permute-done.2.refs_1_, bf16[64,1024]{1,0:T(8,128)(2,1)S(1)} %collective-permute-done.3.refs_2_, bf16[64,1024]{1,0:T(8,128)(2,1)S(1)} %collective-permute-done.4.refs_3_, ...), custom_call_target="tpu_custom_call" | custom-call | flops 1000000000 | bytes 1048576 | tf_op jit(solution)/shard_map/pallas_call | solution.py:22
  34.4 2.7 %collective-permute-done.11.third_ref = bf16[512,256]{1,0:T(8,128)(2,1)S(1)} collective-permute-done((bf16[512,256]{1,0:T(8,128)(2,1)S(1)}, bf16[512,256]{1,0:T(8,128)(2,1)S(1)}, u32[]{:S(2)}, u32[]{:S(2)}) %collective-permute-start.11) | collective-permute-done | bytes 262176 | tf_op jit(solution)/shard_map/ppermute | solution.py:252
  37.0 2.3 %collective-permute-done.10.second_ref = bf16[512,256]{1,0:T(8,128)(2,1)S(1)} collective-permute-done((bf16[512,256]{1,0:T(8,128)(2,1)S(1)}, bf16[512,256]{1,0:T(8,128)(2,1)S(1)}, u32[]{:S(2)}, u32[]{:S(2)}) %collective-permute-start.10) | collective-permute-done | bytes 262176 | tf_op jit(solution)/shard_map/ppermute | solution.py:252
  39.3 2.7 %collective-permute-done.9.first_ref = bf16[512,256]{1,0:T(8,128)(2,1)S(1)} collective-permute-done((bf16[512,256]{1,0:T(8,128)(2,1)S(1)}, bf16[512,256]{1,0:T(8,128)(2,1)S(1)}, u32[]{:S(2)}, u32[]{:S(2)}) %collective-permute-start.9) | collective-permute-done | bytes 262176 | tf_op jit(solution)/shard_map/ppermute | solution.py:252
  42.4 3.3 %collective-permute-start.13 = (bf16[2,128,256]{2,1,0:T(8,128)(2,1)S(1)}, bf16[2,128,256]{2,1,0:T(8,128)(2,1)S(1)}, u32[]{:S(2)}, u32[]{:S(2)}) collective-permute-start(bf16[2,128,256]{2,1,0:T(8,128)(2,1)S(1)} %get-tuple-element.23), channel_id=1, source_target_pairs={{0,64},{1,9},{2,66},{3,11},{64,0},{65,73},{66,2},{67,75},{4,68},{5... | collective-permute-start | bytes 393224 | tf_op jit(solution)/shard_map/ppermute | solution.py:252
  45.7 2.5 %collective-permute-start.14 = (bf16[2,128,256]{2,1,0:T(8,128)(2,1)S(1)}, bf16[2,128,256]{2,1,0:T(8,128)(2,1)S(1)}, u32[]{:S(2)}, u32[]{:S(2)}) collective-permute-start(bf16[2,128,256]{2,1,0:T(8,128)(2,1)S(1)} %get-tuple-element.24), channel_id=1, source_target_pairs={{0,66},{1,13},{2,0},{3,15},{64,2},{65,77},{66,64},{67,79},{4,70},{... | collective-permute-start | bytes 393224 | tf_op jit(solution)/shard_map/ppermute | solution.py:252
  49.1 0.9 %collective-permute-done.13.second_ref = bf16[2,128,256]{2,1,0:T(8,128)(2,1)S(1)} collective-permute-done((bf16[2,128,256]{2,1,0:T(8,128)(2,1)S(1)}, bf16[2,128,256]{2,1,0:T(8,128)(2,1)S(1)}, u32[]{:S(2)}, u32[]{:S(2)}) %collective-permute-start.13) | collective-permute-done | bytes 131104 | tf_op jit(solution)/shard_map/ppermute | solution.py:252
  50.0 0.9 %collective-permute-done.14.third_ref = bf16[2,128,256]{2,1,0:T(8,128)(2,1)S(1)} collective-permute-done((bf16[2,128,256]{2,1,0:T(8,128)(2,1)S(1)}, bf16[2,128,256]{2,1,0:T(8,128)(2,1)S(1)}, u32[]{:S(2)}, u32[]{:S(2)}) %collective-permute-start.14) | collective-permute-done | bytes 131104 | tf_op jit(solution)/shard_map/ppermute | solution.py:252
  50.8 0.9 %shard_map.58 = f32[128,512]{1,0:T(8,128)} custom-call(f32[2,128,256]{2,1,0:T(8,128)S(1)} %get-tuple-element.21.own_ref, bf16[2,128,256]{2,1,0:T(8,128)(2,1)S(1)} %collective-permute-done.12.first_ref, bf16[2,128,256]{2,1,0:T(8,128)(2,1)S(1)} %collective-permute-done.13.second_ref, bf16[2,128,256]{2,1,0:T(8,128)(2,1)S(1)} %collective-permute-done.14.third_ref, ...), custom_call_target="tpu_custom_call" | custom-call | flops 100000000 | bytes 1048576 | tf_op jit(solution)/shard_map/pallas_call | solution.py:22
  (31 shorter events, 6.3 us)
Async XLA Ops:
  0.0 3.7 %collective-permute-start = (f32[64,1024]{1,0:T(8,128)}, f32[64,1024]{1,0:T(8,128)S(1)}, u32[]{:S(2)}, u32[]{:S(2)}) collective-permute-start(f32[64,1024]{1,0:T(8,128)} %own_ref.1), channel_id=1, source_target_pairs={{0,1},{1,0},{2,3},{3,2},{4,5},{5,4},{6,7},{7,6},{8,9},{9,8},{10,11... | collective-permute-start | bytes 786440 | tf_op jit(solution)/shard_map/ppermute | solution.py:257
  1.0 2.6 %collective-permute-start.1 = (f16[64,640]{1,0:T(8,128)(2,1)S(1)}, f16[64,640]{1,0:T(8,128)(2,1)S(1)}, u32[]{:S(2)}, u32[]{:S(2)}) collective-permute-start(f16[64,640]{1,0:T(8,128)(2,1)S(1)} %multiply_convert_fusion), channel_id=1, source_target_pairs={{1,2},{3,4},{5,6},{7,8},{9,10},{11,12},{13,14},{2,1},{4,3},{6,5},{... | collective-permute-start | bytes 245768 | tf_op jit(solution)/shard_map/ppermute | solution.py:270
  1.7 1.0 %copy-start = (f32[64,1024]{1,0:T(8,128)S(1)}, f32[64,1024]{1,0:T(8,128)}, u32[]{:S(2)}) copy-start(f32[64,1024]{1,0:T(8,128)} %own_ref.1) | copy-start | bytes 786436
  2.7 0.7 %copy-start.2 = (f32[1024]{0:T(1024)S(1)}, f32[1024]{0:T(1024)}, u32[]{:S(2)}) copy-start(f32[1024]{0:T(1024)} %param.5) | copy-start | bytes 12292
  4.5 11.5 %collective-permute-start.2 = (bf16[64,1024]{1,0:T(8,128)(2,1)S(1)}, bf16[64,1024]{1,0:T(8,128)(2,1)S(1)}, u32[]{:S(2)}, u32[]{:S(2)}) collective-permute-start(bf16[64,1024]{1,0:T(8,128)(2,1)S(1)} %get-tuple-element.19.refs_0_), channel_id=1, source_target_pairs={{0,48},{16,0},{32,16},{48,32},{1,49},{17,1},{33,17},{49,33},{2,50}... | collective-permute-start | bytes 393224 | tf_op jit(solution)/shard_map/ppermute | solution.py:257
  8.7 7.3 %collective-permute-start.3 = (bf16[64,1024]{1,0:T(8,128)(2,1)S(1)}, bf16[64,1024]{1,0:T(8,128)(2,1)S(1)}, u32[]{:S(2)}, u32[]{:S(2)}) collective-permute-start(bf16[64,1024]{1,0:T(8,128)(2,1)S(1)} %get-tuple-element.19.refs_0_), channel_id=1, source_target_pairs={{0,32},{16,48},{32,0},{48,16},{1,33},{17,49},{33,1},{49,17},{2,34}... | collective-permute-start | bytes 393224 | tf_op jit(solution)/shard_map/ppermute | solution.py:257
  8.7 9.4 %collective-permute-start.4 = (bf16[64,1024]{1,0:T(8,128)(2,1)S(1)}, bf16[64,1024]{1,0:T(8,128)(2,1)S(1)}, u32[]{:S(2)}, u32[]{:S(2)}) collective-permute-start(bf16[64,1024]{1,0:T(8,128)(2,1)S(1)} %get-tuple-element.19.refs_0_), channel_id=1, source_target_pairs={{0,16},{16,32},{32,48},{48,0},{1,17},{17,33},{33,49},{49,1},{2,18}... | collective-permute-start | bytes 393224 | tf_op jit(solution)/shard_map/ppermute | solution.py:257
  10.0 11.0 %collective-permute-start.5 = (bf16[64,1152]{1,0:T(8,128)(2,1)S(1)}, bf16[64,1152]{1,0:T(8,128)(2,1)S(1)}, u32[]{:S(2)}, u32[]{:S(2)}) collective-permute-start(bf16[64,1152]{1,0:T(8,128)(2,1)S(1)} %get-tuple-element.20.segment_ref), channel_id=1, source_target_pairs={{0,1},{1,0},{2,3},{3,2},{4,5},{5,4},{6,7},{7,6},{8,9},{9,8},{10,11... | collective-permute-start | bytes 442376 | tf_op jit(solution)/shard_map/ppermute | solution.py:257
  12.8 7.3 %collective-permute-start.7 = (bf16[64,1152]{1,0:T(8,128)(2,1)S(1)}, bf16[64,1152]{1,0:T(8,128)(2,1)S(1)}, u32[]{:S(2)}, u32[]{:S(2)}) collective-permute-start(bf16[64,1152]{1,0:T(8,128)(2,1)S(1)} %get-tuple-element.20.segment_ref), channel_id=1, source_target_pairs={{0,64},{64,0},{1,65},{65,1},{2,66},{66,2},{3,67},{67,3},{4,68},{68... | collective-permute-start | bytes 442376 | tf_op jit(solution)/shard_map/ppermute | solution.py:257
  18.1 4.9 %collective-permute-start.6 = (bf16[192,1024]{1,0:T(8,128)(2,1)S(1)}, bf16[192,1024]{1,0:T(8,128)(2,1)S(1)}, u32[]{:S(2)}, u32[]{:S(2)}) collective-permute-start(bf16[192,1024]{1,0:T(8,128)(2,1)S(1)} %pad_maximum_fusion), channel_id=1, source_target_pairs={{0,1},{1,0},{2,3},{3,2},{4,5},{5,4},{6,7},{7,6},{8,9},{9,8},{10,11... | collective-permute-start | bytes 1179656 | tf_op jit(solution)/shard_map/ppermute | solution.py:257
  20.1 2.1 %collective-permute-start.8 = (bf16[64,1152]{1,0:T(8,128)(2,1)S(1)}, bf16[64,1152]{1,0:T(8,128)(2,1)S(1)}, u32[]{:S(2)}, u32[]{:S(2)}) collective-permute-start(bf16[64,1152]{1,0:T(8,128)(2,1)S(1)} %collective-permute-done.7.segment_ref), channel_id=1, source_target_pairs={{0,1},{1,0},{2,3},{3,2},{4,5},{5,4},{6,7},{7,6},{8,9},{9,8},{10,11... | collective-permute-start | bytes 442376 | tf_op jit(solution)/shard_map/ppermute | solution.py:257
  23.8 13.2 %collective-permute-start.11 = (bf16[512,256]{1,0:T(8,128)(2,1)S(1)}, bf16[512,256]{1,0:T(8,128)(2,1)S(1)}, u32[]{:S(2)}, u32[]{:S(2)}) collective-permute-start(bf16[512,256]{1,0:T(8,128)(2,1)S(1)} %shard_map.56), channel_id=1, source_target_pairs={{0,12},{1,67},{2,14},{3,1},{64,76},{65,3},{66,78},{67,65},{4,0},{5... | collective-permute-start | bytes 786440 | tf_op jit(solution)/shard_map/ppermute | solution.py:252
  31.1 8.2 %collective-permute-start.10 = (bf16[512,256]{1,0:T(8,128)(2,1)S(1)}, bf16[512,256]{1,0:T(8,128)(2,1)S(1)}, u32[]{:S(2)}, u32[]{:S(2)}) collective-permute-start(bf16[512,256]{1,0:T(8,128)(2,1)S(1)} %shard_map.55), channel_id=1, source_target_pairs={{0,8},{1,65},{2,10},{3,67},{64,72},{65,1},{66,74},{67,3},{4,12},{5... | collective-permute-start | bytes 786440 | tf_op jit(solution)/shard_map/ppermute | solution.py:252
  32.6 9.4 %collective-permute-start.9 = (bf16[512,256]{1,0:T(8,128)(2,1)S(1)}, bf16[512,256]{1,0:T(8,128)(2,1)S(1)}, u32[]{:S(2)}, u32[]{:S(2)}) collective-permute-start(bf16[512,256]{1,0:T(8,128)(2,1)S(1)} %shard_map.54), channel_id=1, source_target_pairs={{0,4},{1,3},{2,6},{3,65},{64,68},{65,67},{66,70},{67,1},{4,8},{5,7... | collective-permute-start | bytes 786440 | tf_op jit(solution)/shard_map/ppermute | solution.py:252
  34.3 16.5 %copy-start.1 = (f32[2,64,512]{2,1,0:T(8,128)S(1)}, f32[2,64,512]{2,1,0:T(8,128)}, u32[]{:S(2)}) copy-start(f32[2,64,512]{2,1,0:T(8,128)} %param.7) | copy-start | bytes 786436
  42.3 6.8 %collective-permute-start.12 = (bf16[2,128,256]{2,1,0:T(8,128)(2,1)S(1)}, bf16[2,128,256]{2,1,0:T(8,128)(2,1)S(1)}, u32[]{:S(2)}, u32[]{:S(2)}) collective-permute-start(bf16[2,128,256]{2,1,0:T(8,128)(2,1)S(1)} %get-tuple-element.22), channel_id=1, source_target_pairs={{0,2},{1,5},{2,64},{3,7},{64,66},{65,69},{66,0},{67,71},{4,6},{5,9... | collective-permute-start | bytes 393224 | tf_op jit(solution)/shard_map/ppermute | solution.py:252
  42.4 7.6 %collective-permute-start.13 = (bf16[2,128,256]{2,1,0:T(8,128)(2,1)S(1)}, bf16[2,128,256]{2,1,0:T(8,128)(2,1)S(1)}, u32[]{:S(2)}, u32[]{:S(2)}) collective-permute-start(bf16[2,128,256]{2,1,0:T(8,128)(2,1)S(1)} %get-tuple-element.23), channel_id=1, source_target_pairs={{0,64},{1,9},{2,66},{3,11},{64,0},{65,73},{66,2},{67,75},{4,68},{5... | collective-permute-start | bytes 393224 | tf_op jit(solution)/shard_map/ppermute | solution.py:252
  45.7 5.1 %collective-permute-start.14 = (bf16[2,128,256]{2,1,0:T(8,128)(2,1)S(1)}, bf16[2,128,256]{2,1,0:T(8,128)(2,1)S(1)}, u32[]{:S(2)}, u32[]{:S(2)}) collective-permute-start(bf16[2,128,256]{2,1,0:T(8,128)(2,1)S(1)} %get-tuple-element.24), channel_id=1, source_target_pairs={{0,66},{1,13},{2,0},{3,15},{64,2},{65,77},{66,64},{67,79},{4,70},{... | collective-permute-start | bytes 393224 | tf_op jit(solution)/shard_map/ppermute | solution.py:252

commit v4 on v3

--- a/solution.py
+++ b/solution.py
@@ -99,17 +99,21 @@
 
 def rows_kernel(lag_count, segment_ref, rows_ref):
     channels = segment_ref.shape[0]
-    core = lax.axis_index("c")
-    segment = segment_ref[...]
-    segment = jnp.where(core == 0, segment, pltpu.roll(segment, 2, 1))
     groups = lag_count // 2
-    for index in range(lag_count):
-        group, second = index // 2, index % 2
-        lag = 4 * group + second
-        moved = segment if lag == 0 else pltpu.roll(segment, lag, 1)
-        place = jnp.where(core == 0, group, group % 2 * (groups // 2) + group // 2)
-        at = pl.ds(pl.multiple_of((2 * place + second) * channels, channels), channels)
-        rows_ref[at, :] = moved[:, PAD:]
+
+    def fill(core):
+        for index in range(lag_count):
+            group, second = index // 2, index % 2
+            lag = 4 * group + second + 2 * core
+            place = group % 2 * (groups // 2) + group // 2 if core else group
+            at = (2 * place + second) * channels
+            for k in range(0, channels, 16):
+                strip = segment_ref[k : k + 16, :]
+                moved = pltpu.roll(strip, lag, 1) if lag else strip
+                rows_ref[at + k : at + k + 16, :] = moved[:, PAD:]
+
+    pl.when(lax.axis_index("c") == 0)(lambda: fill(0))
+    pl.when(lax.axis_index("c") != 0)(lambda: fill(1))
 
 
 def lagged_rows(segment, lag_count):
@@ -264,7 +268,7 @@
     lags = old_stack.shape[0]
     core, z, yh, zs = lax.axis_index("c"), lax.axis_index("z"), lax.axis_index("yh"), lax.axis_size("z")
     reach = half_taps + PAD
-    edge = jnp.where(core == 0, raw_strain[:, :reach], raw_strain[:, seg_len - reach :])
+    edge = lax.dynamic_slice_in_dim(raw_strain, core * (seg_len - reach), reach, 1)
     edge = (edge * SCALE).astype(jnp.float16)
     pairs = [(i, i + 1) for i in range(1, segments - 1, 2)]
     across = lax.ppermute(edge, TIME, pairs + [(b, a) for a, b in pairs])

time: 52.4 us -> 51.8 us (0.989)
  transfers between devices with their start and end apart: 15 -> 15, of which waited for: 6 -> 7; matrix products, arithmetic and copies ran while one was open for 4% -> 4% of each run, Pallas kernels for 11% -> 11%
where the time goes in v4:
time: 51.8 us; the launch traced here: 51.2 us
  starting transfers between devices  27.5 us (53%)
  waiting for transfers between devices  11.8 us (23%)
  Pallas kernels  8.3 us (16%)
  local copies, waits for them, and re-layouts  1.79 us (3%)
  other arithmetic  1.67 us (3%)
    ppermute x6, starting transfers between devices, passed(): return lax.ppermute(value, axes, pairs)  14 us
    ppermute x8, starting transfers between devices, turned(): lax.ppermute(value, axis, [(i, (i + distance) % size) for i in range(size)])  12.8 us
    ppermute x6, waiting for transfers between devices, passed(): return lax.ppermute(value, axes, pairs)  9.6 us
    pallas_call x13, Pallas kernels, call(): pl.pallas_call(kernel, out_shape=out_shape, in_specs=[VMEM] * len(operand...  8.3 us
    ppermute x8, waiting for transfers between devices, turned(): lax.ppermute(value, axis, [(i, (i + distance) % size) for i in range(size)])  2.2 us
    unnamed x6, local copies, waits for them, and re-layouts  1.64 us
  transfers between devices with their start and end apart: 15, of which 7 were waited for; matrix products, arithmetic and copies ran while one was open for 4% of the time, Pallas kernels for 11%

profile of v4, /device:TPU:0, one launch (start us, length us, event | category | flops | bytes accessed | tf_op | source)
XLA Modules:
  0.0 51.2 jit_solution(13737870236754446641)
XLA Ops:
  0.0 0.9 %multiply_convert_fusion = f16[64,640]{1,0:T(8,128)(2,1)S(1)} fusion(f32[64,1024]{1,0:T(8,128)} %own_ref.1, s32[]{:T(128)S(6)} %select_n.6), kind=kLoop, calls=%fused_computation.2 | loop fusion | flops 81920 | bytes 245764 | tf_op jit(solution)/shard_map/convert_element_type | solution.py:272
  1.6 0.9 %copy-done.1 = f32[64,1024]{1,0:T(8,128)S(1)} copy-done((f32[64,1024]{1,0:T(8,128)S(1)}, f32[64,1024]{1,0:T(8,128)}, u32[]{:S(2)}) %copy-start.1) | copy-done | bytes 262168
  3.6 0.8 %shard_map.47 = (bf16[64,1152]{1,0:T(8,128)(2,1)S(1)}, bf16[64,1024]{1,0:T(8,128)(2,1)S(1)}) custom-call(f32[64,1024]{1,0:T(8,128)S(1)} %collective-permute-done.beside_ref, f32[64,640]{1,0:T(8,128)S(1)} %convert_multiply_fusion.across_ref, bf16[256,1280]{1,0:T(8,128)(2,1)S(1)} %get-tuple-element.15.mat_high_ref, ...), custom_call_target="tpu_custom_call" | custom-call | flops 1000000000 | bytes 1048576 | tf_op jit(solution)/shard_map/pallas_call | solution.py:22
  4.4 4.2 %collective-permute-start.2 = (bf16[64,1024]{1,0:T(8,128)(2,1)S(1)}, bf16[64,1024]{1,0:T(8,128)(2,1)S(1)}, u32[]{:S(2)}, u32[]{:S(2)}) collective-permute-start(bf16[64,1024]{1,0:T(8,128)(2,1)S(1)} %get-tuple-element.19.refs_0_), channel_id=1, source_target_pairs={{0,48},{16,0},{32,16},{48,32},{1,49},{17,1},{33,17},{49,33},{2,50}... | collective-permute-start | bytes 393224 | tf_op jit(solution)/shard_map/ppermute | solution.py:261
  8.6 1.3 %collective-permute-start.4 = (bf16[64,1024]{1,0:T(8,128)(2,1)S(1)}, bf16[64,1024]{1,0:T(8,128)(2,1)S(1)}, u32[]{:S(2)}, u32[]{:S(2)}) collective-permute-start(bf16[64,1024]{1,0:T(8,128)(2,1)S(1)} %get-tuple-element.19.refs_0_), channel_id=1, source_target_pairs={{0,16},{16,32},{32,48},{48,0},{1,17},{17,33},{33,49},{49,1},{2,18}... | collective-permute-start | bytes 393224 | tf_op jit(solution)/shard_map/ppermute | solution.py:261
  9.9 2.8 %collective-permute-start.5 = (bf16[64,1152]{1,0:T(8,128)(2,1)S(1)}, bf16[64,1152]{1,0:T(8,128)(2,1)S(1)}, u32[]{:S(2)}, u32[]{:S(2)}) collective-permute-start(bf16[64,1152]{1,0:T(8,128)(2,1)S(1)} %get-tuple-element.20.segment_ref), channel_id=1, source_target_pairs={{0,1},{1,0},{2,3},{3,2},{4,5},{5,4},{6,7},{7,6},{8,9},{9,8},{10,11... | collective-permute-start | bytes 442376 | tf_op jit(solution)/shard_map/ppermute | solution.py:261
  12.7 3.2 %collective-permute-start.7 = (bf16[64,1152]{1,0:T(8,128)(2,1)S(1)}, bf16[64,1152]{1,0:T(8,128)(2,1)S(1)}, u32[]{:S(2)}, u32[]{:S(2)}) collective-permute-start(bf16[64,1152]{1,0:T(8,128)(2,1)S(1)} %get-tuple-element.20.segment_ref), channel_id=1, source_target_pairs={{0,64},{64,0},{1,65},{65,1},{2,66},{66,2},{3,67},{67,3},{4,68},{68... | collective-permute-start | bytes 442376 | tf_op jit(solution)/shard_map/ppermute | solution.py:261
  15.9 2.1 %collective-permute-done.4.refs_3_ = bf16[64,1024]{1,0:T(8,128)(2,1)S(1)} collective-permute-done((bf16[64,1024]{1,0:T(8,128)(2,1)S(1)}, bf16[64,1024]{1,0:T(8,128)(2,1)S(1)}, u32[]{:S(2)}, u32[]{:S(2)}) %collective-permute-start.4) | collective-permute-done | bytes 131104 | tf_op jit(solution)/shard_map/ppermute | solution.py:261
  18.1 1.2 %collective-permute-start.6 = (bf16[192,1024]{1,0:T(8,128)(2,1)S(1)}, bf16[192,1024]{1,0:T(8,128)(2,1)S(1)}, u32[]{:S(2)}, u32[]{:S(2)}) collective-permute-start(bf16[192,1024]{1,0:T(8,128)(2,1)S(1)} %pad_maximum_fusion), channel_id=1, source_target_pairs={{0,1},{1,0},{2,3},{3,2},{4,5},{5,4},{6,7},{7,6},{8,9},{9,8},{10,11... | collective-permute-start | bytes 1179656 | tf_op jit(solution)/shard_map/ppermute | solution.py:261
  22.5 0.8 %shard_map.56 = bf16[512,256]{1,0:T(8,128)(2,1)S(1)} custom-call(bf16[64,1024]{1,0:T(8,128)(2,1)S(1)} %get-tuple-element.19.refs_0_, bf16[64,1024]{1,0:T(8,128)(2,1)S(1)} %collective-permute-done.2.refs_1_, bf16[64,1024]{1,0:T(8,128)(2,1)S(1)} %collective-permute-done.3.refs_2_, bf16[64,1024]{1,0:T(8,128)(2,1)S(1)} %collective-permute-done.4.refs_3_, ...), custom_call_target="tpu_custom_call" | custom-call | flops 1000000000 | bytes 1048576 | tf_op jit(solution)/shard_map/pallas_call | solution.py:22
  23.3 6.5 %collective-permute-start.11 = (bf16[512,256]{1,0:T(8,128)(2,1)S(1)}, bf16[512,256]{1,0:T(8,128)(2,1)S(1)}, u32[]{:S(2)}, u32[]{:S(2)}) collective-permute-start(bf16[512,256]{1,0:T(8,128)(2,1)S(1)} %shard_map.56), channel_id=1, source_target_pairs={{0,12},{1,67},{2,14},{3,1},{64,76},{65,3},{66,78},{67,65},{4,0},{5... | collective-permute-start | bytes 786440 | tf_op jit(solution)/shard_map/ppermute | solution.py:256
  29.8 0.9 %shard_map.55 = bf16[512,256]{1,0:T(8,128)(2,1)S(1)} custom-call(bf16[64,1024]{1,0:T(8,128)(2,1)S(1)} %get-tuple-element.19.refs_0_, bf16[64,1024]{1,0:T(8,128)(2,1)S(1)} %collective-permute-done.2.refs_1_, bf16[64,1024]{1,0:T(8,128)(2,1)S(1)} %collective-permute-done.3.refs_2_, bf16[64,1024]{1,0:T(8,128)(2,1)S(1)} %collective-permute-done.4.refs_3_, ...), custom_call_target="tpu_custom_call" | custom-call | flops 1000000000 | bytes 1048576 | tf_op jit(solution)/shard_map/pallas_call | solution.py:22
  30.8 0.9 %collective-permute-start.10 = (bf16[512,256]{1,0:T(8,128)(2,1)S(1)}, bf16[512,256]{1,0:T(8,128)(2,1)S(1)}, u32[]{:S(2)}, u32[]{:S(2)}) collective-permute-start(bf16[512,256]{1,0:T(8,128)(2,1)S(1)} %shard_map.55), channel_id=1, source_target_pairs={{0,8},{1,65},{2,10},{3,67},{64,72},{65,1},{66,74},{67,3},{4,12},{5... | collective-permute-start | bytes 786440 | tf_op jit(solution)/shard_map/ppermute | solution.py:256
  32.1 1.0 %collective-permute-start.9 = (bf16[512,256]{1,0:T(8,128)(2,1)S(1)}, bf16[512,256]{1,0:T(8,128)(2,1)S(1)}, u32[]{:S(2)}, u32[]{:S(2)}) collective-permute-start(bf16[512,256]{1,0:T(8,128)(2,1)S(1)} %shard_map.54), channel_id=1, source_target_pairs={{0,4},{1,3},{2,6},{3,65},{64,68},{65,67},{66,70},{67,1},{4,8},{5,7... | collective-permute-start | bytes 786440 | tf_op jit(solution)/shard_map/ppermute | solution.py:256
  33.1 0.8 %shard_map.52.own_ref = f32[512,256]{1,0:T(8,128)S(1)} custom-call(bf16[64,1024]{1,0:T(8,128)(2,1)S(1)} %get-tuple-element.19.refs_0_, bf16[64,1024]{1,0:T(8,128)(2,1)S(1)} %collective-permute-done.2.refs_1_, bf16[64,1024]{1,0:T(8,128)(2,1)S(1)} %collective-permute-done.3.refs_2_, bf16[64,1024]{1,0:T(8,128)(2,1)S(1)} %collective-permute-done.4.refs_3_, ...), custom_call_target="tpu_custom_call" | custom-call | flops 1000000000 | bytes 1048576 | tf_op jit(solution)/shard_map/pallas_call | solution.py:22
  33.9 2.7 %collective-permute-done.11.third_ref = bf16[512,256]{1,0:T(8,128)(2,1)S(1)} collective-permute-done((bf16[512,256]{1,0:T(8,128)(2,1)S(1)}, bf16[512,256]{1,0:T(8,128)(2,1)S(1)}, u32[]{:S(2)}, u32[]{:S(2)}) %collective-permute-start.11) | collective-permute-done | bytes 262176 | tf_op jit(solution)/shard_map/ppermute | solution.py:256
  36.5 2.3 %collective-permute-done.10.second_ref = bf16[512,256]{1,0:T(8,128)(2,1)S(1)} collective-permute-done((bf16[512,256]{1,0:T(8,128)(2,1)S(1)}, bf16[512,256]{1,0:T(8,128)(2,1)S(1)}, u32[]{:S(2)}, u32[]{:S(2)}) %collective-permute-start.10) | collective-permute-done | bytes 262176 | tf_op jit(solution)/shard_map/ppermute | solution.py:256
  38.8 2.7 %collective-permute-done.9.first_ref = bf16[512,256]{1,0:T(8,128)(2,1)S(1)} collective-permute-done((bf16[512,256]{1,0:T(8,128)(2,1)S(1)}, bf16[512,256]{1,0:T(8,128)(2,1)S(1)}, u32[]{:S(2)}, u32[]{:S(2)}) %collective-permute-start.9) | collective-permute-done | bytes 262176 | tf_op jit(solution)/shard_map/ppermute | solution.py:256
  41.9 3.1 %collective-permute-start.13 = (bf16[2,128,256]{2,1,0:T(8,128)(2,1)S(1)}, bf16[2,128,256]{2,1,0:T(8,128)(2,1)S(1)}, u32[]{:S(2)}, u32[]{:S(2)}) collective-permute-start(bf16[2,128,256]{2,1,0:T(8,128)(2,1)S(1)} %get-tuple-element.23), channel_id=1, source_target_pairs={{0,64},{1,9},{2,66},{3,11},{64,0},{65,73},{66,2},{67,75},{4,68},{5... | collective-permute-start | bytes 393224 | tf_op jit(solution)/shard_map/ppermute | solution.py:256
  45.0 2.5 %collective-permute-start.14 = (bf16[2,128,256]{2,1,0:T(8,128)(2,1)S(1)}, bf16[2,128,256]{2,1,0:T(8,128)(2,1)S(1)}, u32[]{:S(2)}, u32[]{:S(2)}) collective-permute-start(bf16[2,128,256]{2,1,0:T(8,128)(2,1)S(1)} %get-tuple-element.24), channel_id=1, source_target_pairs={{0,66},{1,13},{2,0},{3,15},{64,2},{65,77},{66,64},{67,79},{4,70},{... | collective-permute-start | bytes 393224 | tf_op jit(solution)/shard_map/ppermute | solution.py:256
  47.5 0.7 %multiply_bitcast_fusion = f32[8]{0:T(128)S(1)} fusion(s32[8,8]{1,0:T(8,128)} %param.6, s32[]{:T(128)S(6)} %select_n.7), kind=kLoop, calls=%fused_computation.3 | loop fusion | flops 16 | bytes 68 | tf_op jit(solution)/shard_map/mul | solution.py:299
  48.4 1.1 %collective-permute-done.12.first_ref = bf16[2,128,256]{2,1,0:T(8,128)(2,1)S(1)} collective-permute-done((bf16[2,128,256]{2,1,0:T(8,128)(2,1)S(1)}, bf16[2,128,256]{2,1,0:T(8,128)(2,1)S(1)}, u32[]{:S(2)}, u32[]{:S(2)}) %collective-permute-start.12) | collective-permute-done | bytes 131104 | tf_op jit(solution)/shard_map/ppermute | solution.py:256
  49.5 0.9 %collective-permute-done.14.third_ref = bf16[2,128,256]{2,1,0:T(8,128)(2,1)S(1)} collective-permute-done((bf16[2,128,256]{2,1,0:T(8,128)(2,1)S(1)}, bf16[2,128,256]{2,1,0:T(8,128)(2,1)S(1)}, u32[]{:S(2)}, u32[]{:S(2)}) %collective-permute-start.14) | collective-permute-done | bytes 131104 | tf_op jit(solution)/shard_map/ppermute | solution.py:256
  50.3 0.9 %shard_map.58 = f32[128,512]{1,0:T(8,128)} custom-call(f32[2,128,256]{2,1,0:T(8,128)S(1)} %get-tuple-element.21.own_ref, bf16[2,128,256]{2,1,0:T(8,128)(2,1)S(1)} %collective-permute-done.12.first_ref, bf16[2,128,256]{2,1,0:T(8,128)(2,1)S(1)} %collective-permute-done.13.second_ref, bf16[2,128,256]{2,1,0:T(8,128)(2,1)S(1)} %collective-permute-done.14.third_ref, ...), custom_call_target="tpu_custom_call" | custom-call | flops 100000000 | bytes 1048576 | tf_op jit(solution)/shard_map/pallas_call | solution.py:22
  (31 shorter events, 5.9 us)
Async XLA Ops:
  0.0 3.6 %collective-permute-start = (f32[64,1024]{1,0:T(8,128)}, f32[64,1024]{1,0:T(8,128)S(1)}, u32[]{:S(2)}, u32[]{:S(2)}) collective-permute-start(f32[64,1024]{1,0:T(8,128)} %own_ref.1), channel_id=1, source_target_pairs={{0,1},{1,0},{2,3},{3,2},{4,5},{5,4},{6,7},{7,6},{8,9},{9,8},{10,11... | collective-permute-start | bytes 786440 | tf_op jit(solution)/shard_map/ppermute | solution.py:261
  0.9 2.6 %collective-permute-start.1 = (f16[64,640]{1,0:T(8,128)(2,1)S(1)}, f16[64,640]{1,0:T(8,128)(2,1)S(1)}, u32[]{:S(2)}, u32[]{:S(2)}) collective-permute-start(f16[64,640]{1,0:T(8,128)(2,1)S(1)} %multiply_convert_fusion), channel_id=1, source_target_pairs={{1,2},{3,4},{5,6},{7,8},{9,10},{11,12},{13,14},{2,1},{4,3},{6,5},{... | collective-permute-start | bytes 245768 | tf_op jit(solution)/shard_map/ppermute | solution.py:274
  1.6 1.0 %copy-start.1 = (f32[64,1024]{1,0:T(8,128)S(1)}, f32[64,1024]{1,0:T(8,128)}, u32[]{:S(2)}) copy-start(f32[64,1024]{1,0:T(8,128)} %own_ref.1) | copy-start | bytes 786436
  2.6 0.7 %copy-start.2 = (f32[1024]{0:T(1024)S(1)}, f32[1024]{0:T(1024)}, u32[]{:S(2)}) copy-start(f32[1024]{0:T(1024)} %param.5) | copy-start | bytes 12292
  4.4 11.5 %collective-permute-start.2 = (bf16[64,1024]{1,0:T(8,128)(2,1)S(1)}, bf16[64,1024]{1,0:T(8,128)(2,1)S(1)}, u32[]{:S(2)}, u32[]{:S(2)}) collective-permute-start(bf16[64,1024]{1,0:T(8,128)(2,1)S(1)} %get-tuple-element.19.refs_0_), channel_id=1, source_target_pairs={{0,48},{16,0},{32,16},{48,32},{1,49},{17,1},{33,17},{49,33},{2,50}... | collective-permute-start | bytes 393224 | tf_op jit(solution)/shard_map/ppermute | solution.py:261
  8.6 7.3 %collective-permute-start.3 = (bf16[64,1024]{1,0:T(8,128)(2,1)S(1)}, bf16[64,1024]{1,0:T(8,128)(2,1)S(1)}, u32[]{:S(2)}, u32[]{:S(2)}) collective-permute-start(bf16[64,1024]{1,0:T(8,128)(2,1)S(1)} %get-tuple-element.19.refs_0_), channel_id=1, source_target_pairs={{0,32},{16,48},{32,0},{48,16},{1,33},{17,49},{33,1},{49,17},{2,34}... | collective-permute-start | bytes 393224 | tf_op jit(solution)/shard_map/ppermute | solution.py:261
  8.6 9.4 %collective-permute-start.4 = (bf16[64,1024]{1,0:T(8,128)(2,1)S(1)}, bf16[64,1024]{1,0:T(8,128)(2,1)S(1)}, u32[]{:S(2)}, u32[]{:S(2)}) collective-permute-start(bf16[64,1024]{1,0:T(8,128)(2,1)S(1)} %get-tuple-element.19.refs_0_), channel_id=1, source_target_pairs={{0,16},{16,32},{32,48},{48,0},{1,17},{17,33},{33,49},{49,1},{2,18}... | collective-permute-start | bytes 393224 | tf_op jit(solution)/shard_map/ppermute | solution.py:261
  9.9 10.8 %collective-permute-start.5 = (bf16[64,1152]{1,0:T(8,128)(2,1)S(1)}, bf16[64,1152]{1,0:T(8,128)(2,1)S(1)}, u32[]{:S(2)}, u32[]{:S(2)}) collective-permute-start(bf16[64,1152]{1,0:T(8,128)(2,1)S(1)} %get-tuple-element.20.segment_ref), channel_id=1, source_target_pairs={{0,1},{1,0},{2,3},{3,2},{4,5},{5,4},{6,7},{7,6},{8,9},{9,8},{10,11... | collective-permute-start | bytes 442376 | tf_op jit(solution)/shard_map/ppermute | solution.py:261
  12.7 7.3 %collective-permute-start.7 = (bf16[64,1152]{1,0:T(8,128)(2,1)S(1)}, bf16[64,1152]{1,0:T(8,128)(2,1)S(1)}, u32[]{:S(2)}, u32[]{:S(2)}) collective-permute-start(bf16[64,1152]{1,0:T(8,128)(2,1)S(1)} %get-tuple-element.20.segment_ref), channel_id=1, source_target_pairs={{0,64},{64,0},{1,65},{65,1},{2,66},{66,2},{3,67},{67,3},{4,68},{68... | collective-permute-start | bytes 442376 | tf_op jit(solution)/shard_map/ppermute | solution.py:261
  18.1 4.5 %collective-permute-start.6 = (bf16[192,1024]{1,0:T(8,128)(2,1)S(1)}, bf16[192,1024]{1,0:T(8,128)(2,1)S(1)}, u32[]{:S(2)}, u32[]{:S(2)}) collective-permute-start(bf16[192,1024]{1,0:T(8,128)(2,1)S(1)} %pad_maximum_fusion), channel_id=1, source_target_pairs={{0,1},{1,0},{2,3},{3,2},{4,5},{5,4},{6,7},{7,6},{8,9},{9,8},{10,11... | collective-permute-start | bytes 1179656 | tf_op jit(solution)/shard_map/ppermute | solution.py:261
  20.0 1.9 %collective-permute-start.8 = (bf16[64,1152]{1,0:T(8,128)(2,1)S(1)}, bf16[64,1152]{1,0:T(8,128)(2,1)S(1)}, u32[]{:S(2)}, u32[]{:S(2)}) collective-permute-start(bf16[64,1152]{1,0:T(8,128)(2,1)S(1)} %collective-permute-done.7.segment_ref), channel_id=1, source_target_pairs={{0,1},{1,0},{2,3},{3,2},{4,5},{5,4},{6,7},{7,6},{8,9},{9,8},{10,11... | collective-permute-start | bytes 442376 | tf_op jit(solution)/shard_map/ppermute | solution.py:261
  23.3 13.2 %collective-permute-start.11 = (bf16[512,256]{1,0:T(8,128)(2,1)S(1)}, bf16[512,256]{1,0:T(8,128)(2,1)S(1)}, u32[]{:S(2)}, u32[]{:S(2)}) collective-permute-start(bf16[512,256]{1,0:T(8,128)(2,1)S(1)} %shard_map.56), channel_id=1, source_target_pairs={{0,12},{1,67},{2,14},{3,1},{64,76},{65,3},{66,78},{67,65},{4,0},{5... | collective-permute-start | bytes 786440 | tf_op jit(solution)/shard_map/ppermute | solution.py:256
  30.8 8.1 %collective-permute-start.10 = (bf16[512,256]{1,0:T(8,128)(2,1)S(1)}, bf16[512,256]{1,0:T(8,128)(2,1)S(1)}, u32[]{:S(2)}, u32[]{:S(2)}) collective-permute-start(bf16[512,256]{1,0:T(8,128)(2,1)S(1)} %shard_map.55), channel_id=1, source_target_pairs={{0,8},{1,65},{2,10},{3,67},{64,72},{65,1},{66,74},{67,3},{4,12},{5... | collective-permute-start | bytes 786440 | tf_op jit(solution)/shard_map/ppermute | solution.py:256
  32.1 9.4 %collective-permute-start.9 = (bf16[512,256]{1,0:T(8,128)(2,1)S(1)}, bf16[512,256]{1,0:T(8,128)(2,1)S(1)}, u32[]{:S(2)}, u32[]{:S(2)}) collective-permute-start(bf16[512,256]{1,0:T(8,128)(2,1)S(1)} %shard_map.54), channel_id=1, source_target_pairs={{0,4},{1,3},{2,6},{3,65},{64,68},{65,67},{66,70},{67,1},{4,8},{5,7... | collective-permute-start | bytes 786440 | tf_op jit(solution)/shard_map/ppermute | solution.py:256
  33.9 16.5 %copy-start = (f32[2,64,512]{2,1,0:T(8,128)S(1)}, f32[2,64,512]{2,1,0:T(8,128)}, u32[]{:S(2)}) copy-start(f32[2,64,512]{2,1,0:T(8,128)} %param.7) | copy-start | bytes 786436
  41.8 7.7 %collective-permute-start.12 = (bf16[2,128,256]{2,1,0:T(8,128)(2,1)S(1)}, bf16[2,128,256]{2,1,0:T(8,128)(2,1)S(1)}, u32[]{:S(2)}, u32[]{:S(2)}) collective-permute-start(bf16[2,128,256]{2,1,0:T(8,128)(2,1)S(1)} %get-tuple-element.22), channel_id=1, source_target_pairs={{0,2},{1,5},{2,64},{3,7},{64,66},{65,69},{66,0},{67,71},{4,6},{5,9... | collective-permute-start | bytes 393224 | tf_op jit(solution)/shard_map/ppermute | solution.py:256
  41.9 7.6 %collective-permute-start.13 = (bf16[2,128,256]{2,1,0:T(8,128)(2,1)S(1)}, bf16[2,128,256]{2,1,0:T(8,128)(2,1)S(1)}, u32[]{:S(2)}, u32[]{:S(2)}) collective-permute-start(bf16[2,128,256]{2,1,0:T(8,128)(2,1)S(1)} %get-tuple-element.23), channel_id=1, source_target_pairs={{0,64},{1,9},{2,66},{3,11},{64,0},{65,73},{66,2},{67,75},{4,68},{5... | collective-permute-start | bytes 393224 | tf_op jit(solution)/shard_map/ppermute | solution.py:256
  45.0 5.3 %collective-permute-start.14 = (bf16[2,128,256]{2,1,0:T(8,128)(2,1)S(1)}, bf16[2,128,256]{2,1,0:T(8,128)(2,1)S(1)}, u32[]{:S(2)}, u32[]{:S(2)}) collective-permute-start(bf16[2,128,256]{2,1,0:T(8,128)(2,1)S(1)} %get-tuple-element.24), channel_id=1, source_target_pairs={{0,66},{1,13},{2,0},{3,15},{64,2},{65,77},{66,64},{67,79},{4,70},{... | collective-permute-start | bytes 393224 | tf_op jit(solution)/shard_map/ppermute | solution.py:256
